TPU v7x, 32 devices: a whole 2x2x4 slice. The times are simulated.
32 devices in a mesh: ctx: 16 (over z, y, core), fsdp: 2 (over x).
Axes of the slice: x: 2, y: 2, z: 4, core: 2. Of those that a mesh axis runs over, the one named last changes fastest.
Arguments:
- layer_input: bfloat16 [2, 4096, 768], P('fsdp', 'ctx'), may hold values from -6 to 6
- doc_lengths: int32 [2, 16], P('fsdp'), may hold values from 1 to 2048, 4096 in all within a row
- ln1_gain: bfloat16 [768], P('fsdp'), may hold values from 0.5 to 1.5
- ln1_bias: bfloat16 [768], P('fsdp'), may hold values from -3 to 3
- ln2_gain: bfloat16 [768], P('fsdp'), may hold values from 0.5 to 1.5
- ln2_bias: bfloat16 [768], P('fsdp'), may hold values from -3 to 3
- qkv_weight: bfloat16 [768, 896], P('fsdp'), may hold values from -0.21875 to 0.21875
- qkv_bias: bfloat16 [896], P('fsdp'), may hold values from -3 to 3
- out_weight: bfloat16 [768, 768], P('fsdp'), may hold values from -1 to 1
- out_bias: bfloat16 [768], P('fsdp'), may hold values from -3 to 3
- up_weight: bfloat16 [768, 3072], P('fsdp'), may hold values from -0.21875 to 0.21875
- up_bias: bfloat16 [3072], P('fsdp'), may hold values from -3 to 3
- down_weight: bfloat16 [3072, 768], P('fsdp'), may hold values from -0.109375 to 0.109375
- down_bias: bfloat16 [768], P('fsdp'), may hold values from -3 to 3
- out_grad: bfloat16 [2, 4096, 768], P('fsdp', 'ctx'), may hold values from -6 to 6
- kv_grad_later: float32 [2, 4096, 128], P('fsdp', 'ctx'), may hold values from -8 to 8
Outputs:
- layer_output: bfloat16 [2, 4096, 768], P('fsdp', 'ctx')
- x_grad: float32 [2, 4096, 768], P('fsdp', 'ctx')
- ln1_gain_grad: float32 [768], P('fsdp')
- ln1_bias_grad: float32 [768], P('fsdp')
- ln2_gain_grad: float32 [768], P('fsdp')
- ln2_bias_grad: float32 [768], P('fsdp')
- qkv_weight_grad: float32 [768, 896], P('fsdp')
- qkv_bias_grad: float32 [896], P('fsdp')
- out_weight_grad: float32 [768, 768], P('fsdp')
- out_bias_grad: float32 [768], P('fsdp')
- up_weight_grad: float32 [768, 3072], P('fsdp')
- up_bias_grad: float32 [3072], P('fsdp')
- down_weight_grad: float32 [3072, 768], P('fsdp')
- down_bias_grad: float32 [768], P('fsdp')
Inputs may be any that keep to these rules, and one draw needn't show every extreme that they name: `doc_lengths`: each row lists the 16 documents of one stream in order; they fill its 4096 tokens and the longest has exactly 2048.
All inputs are finite; a program needn't handle non-finite values.
Results may differ from a plain program's by a relative error of at most 0.011.
Values may be sent and summed in bfloat16 or wider, within the bound.
No kernel may reach another device: no remote copies, remote signals or barrier semaphores. Data moves between devices by JAX's collectives and lax.ppermute only.
A program may use at most 192 MiB of HBM per device.

v0:
```python
from functools import partial

import jax
import jax.numpy as jnp
import numpy as np
from jax import lax
from jax.experimental import pallas as pl
from jax.experimental.pallas import tpu as pltpu
from jax.sharding import PartitionSpec as P

ROT = 16
BLOCK = 128
LOW = 16
NT = (((1,), (1,)), ((), ()))
NN = (((1,), (0,)), ((), ()))
TN = (((0,), (0,)), ((), ()))
bf16 = jnp.bfloat16
f32 = jnp.float32
WEIGHT = {'kv_add': 6.0, 'dm_kv': 0.0, 'tail': 3.0, 'tail_sum': 6.0, 'pair': 4.0, 'pair_add': 7.0, 'pair_sum': 7.0, 'pair_join': 7.0, 'both': 7.0, 'both_join': 7.0, 'down_join': 3.0, 'up_out': 0.0, 'up_join': 0.0, 'cotangent': 0.0, 'query': 6.0, 'ff': 0.0, 'attn_backward': 13.0, 'front': 13.0, 'attn_forward': 1.0, 'down_add': 0.0}
TINY = pl.CostEstimate(flops=1, transcendentals=0, bytes_accessed=1)


def mm(left, right, dims=NN):
    return lax.dot_general(left, right, dims, preferred_element_type=f32)


def vmem():
    return pl.BlockSpec(memory_space=pltpu.VMEM)


def smem():
    return pl.BlockSpec(memory_space=pltpu.SMEM)


class Near:
    def __init__(self, value):
        self.value = value


class Raw(Near):
    pass


def near(*values):
    return tuple(Near(v) for v in values)


def call(kernel, name, outs, args, scratch=(), room=2):
    specs = [vmem() for _ in args]
    values = list(args)
    for i, v in enumerate(args):
        if isinstance(v, Raw):
            values[i] = v.value
            specs[i] = pl.BlockSpec(memory_space=pl.ANY)
        elif isinstance(v, Near):
            values[i] = pltpu.with_memory_space_constraint(v.value, pltpu.VMEM)
        elif v.dtype == jnp.int32:
            specs[i] = smem()
    return pl.pallas_call(
        kernel,
        out_shape=tuple(pltpu.VMEM(s, d) if n else jax.ShapeDtypeStruct(s, d) for s, d, n in outs),
        in_specs=specs,
        out_specs=tuple(vmem() for _ in outs),
        scratch_shapes=list(scratch),
        name=name,
        cost_estimate=pl.CostEstimate(
            flops=int(WEIGHT.get(name, 0) * 1e9) + 1, transcendentals=0, bytes_accessed=1
        ),
        compiler_params=pltpu.CompilerParams(vmem_limit_bytes=room << 20),
    )(*values)


def lanes(start, size):
    return pl.ds(pl.multiple_of(start, 128), size)


def swap_x(value):
    return lax.ppermute(value, "fsdp", [(0, 1), (1, 0)])


def swap_ctx(value, mask):
    devices = lax.axis_size("ctx")
    return lax.ppermute(value, "ctx", [(i, i ^ mask) for i in range(devices)])


def stages_of(devices):
    out, stride = [], 1
    while stride < devices:
        out.append((stride, 2))
        stride *= 2
    return out[::-1]


CHUNKS = [int(f"{k:03b}"[::-1], 2) for k in range(8)]


def slot_of(relative, stages):
    slot, count = relative * 0, 1
    for stride, size in stages:
        slot = slot + relative // stride % size * count
        count *= size
    return slot


def join_kernel(*refs):
    out = refs[-1]
    rows = refs[0].shape[0]
    for k, ref in enumerate(refs[:-1]):
        out[k * rows : (k + 1) * rows] = ref[...]


def join(first, second, name):
    shape = (2 * first.shape[0],) + first.shape[1:]
    return call(join_kernel, name, [(shape, first.dtype, True)], near(first, second))[0]


def gather_step(value, mask, name):
    return join(value, swap_ctx(value, mask), name)


def after(value, *others):
    return lax.optimization_barrier((value, *others))[0]


def add_split_kernel(a_ref, b_ref, keep, send):
    half = a_ref.shape[0] // 2
    for ref, part in ((keep, slice(0, half)), (send, slice(half, 2 * half))):
        ref[...] = (a_ref[part].astype(f32) + b_ref[part].astype(f32)).astype(ref.dtype)


def scatter_step(keep, send, mask, name):
    shape = (keep.shape[0] // 2,) + keep.shape[1:]
    out = (shape, keep.dtype, True)
    return call(add_split_kernel, name, [out, out], near(keep, swap_ctx(send, mask)))


def scatter(keep, send, devices, name, stride=1):
    while 2 * stride < devices:
        keep, send = scatter_step(keep, send, stride, name)
        stride *= 2
    return keep, swap_ctx(send, stride)


def high_sum(value):
    devices = lax.axis_size("ctx")
    if devices <= LOW:
        return value
    groups = [[h * LOW + l for h in range(devices // LOW)] for l in range(LOW)]
    return lax.psum(value, "ctx", axis_index_groups=groups)


def pack_kernel(ids, x, dy, kv_w, q_w, up_w, g1, b1, g2, b2, ob, db, qb, small, first, second):
    small[:384, :] = kv_w[...]
    small[384:, :] = jnp.zeros((32, 128), bf16)
    row = 384
    for ref in (g1, b1, g2, b2, ob, db):
        v = ref[...].astype(f32).reshape(1, 384)
        for k in range(3):
            small[row : row + 1, :] = v[:, k * 128 : (k + 1) * 128].astype(bf16)
            row += 1
    v = qb[...].astype(f32).reshape(1, 448)
    for k in range(3):
        small[row + k : row + k + 1, :] = v[:, k * 128 : (k + 1) * 128].astype(bf16)
        small[row + 5 + k : row + 6 + k, :] = v[:, 64 + k * 128 : 64 + (k + 1) * 128].astype(bf16)
    small[row + 3 : row + 4, 0:64] = v[:, 384:448].astype(bf16)
    small[row + 4 : row + 5, 64:128] = v[:, 0:64].astype(bf16)
    first[:416, :] = small[...]
    for k in range(3):
        first[416 + 384 * k : 800 + 384 * k, :] = up_w[:, k * 128 : (k + 1) * 128]
    tokens = x.shape[0]
    second[:tokens] = x[...]
    second[tokens : 2 * tokens] = dy[...]
    rows = q_w.shape[0] // 2
    second[2 * tokens :, : 2 * rows] = q_w[:rows]
    second[2 * tokens :, 2 * rows :] = q_w[rows:]


def pack(ids, x, dy, qkv_weight, up_weight, vectors):
    half, width = qkv_weight.shape[0], 2 * qkv_weight.shape[0]
    tokens = x.shape[0]
    step = up_weight.shape[1] // 8
    token = pl.BlockSpec(x.shape, lambda i, s: (0, 0))
    whole = [pl.BlockSpec(v.shape, lambda i, s: (0,)) for v in vectors]
    outs = ((half + 32, 128), (half + 32 + 3 * half, 128), (2 * tokens + half // 2, width))
    return pl.pallas_call(
        pack_kernel,
        out_shape=tuple(jax.ShapeDtypeStruct(s, bf16) for s in outs),
        grid_spec=pltpu.PrefetchScalarGridSpec(
            num_scalar_prefetch=1,
            grid=(1,),
            in_specs=[
                token,
                token,
                pl.BlockSpec((half, 128), lambda i, s: (0, width // 128)),
                pl.BlockSpec((half, half), lambda i, s: (0, s[2])),
                pl.BlockSpec((half, step), lambda i, s: (0, (1 - s[1]) * 4 + s[2] * 2 + s[3])),
            ]
            + whole,
            out_specs=[pl.BlockSpec(s, lambda i, s: (0, 0)) for s in outs],
        ),
        name="pack",
        cost_estimate=TINY,
    )(ids, x, dy, qkv_weight, qkv_weight, up_weight, *vectors)


def row_vector(block, first, count=3):
    return jnp.concatenate([block[first + k : first + k + 1] for k in range(count)], axis=1)


def natural(side, own, other):
    return jnp.concatenate(
        [jnp.where(side == 0, own, other), jnp.where(side == 0, other, own)], axis=1
    )


def model_vector(side, own, other, index):
    return natural(side, row_vector(own, 3 * index), row_vector(other, 3 * index))


def qkv_bias_tiles(side, own, other):
    low = jnp.where(side == 0, own[18:22], other[18:22])
    high = jnp.where(side == 0, other[22:26], own[22:26])
    tiles = [low[0:1], low[1:2], low[2:3], low[3:4] + high[0:1], high[1:2], high[2:3], high[3:4]]
    return tiles


def normalize(values):
    centred = values - jnp.mean(values, axis=-1, keepdims=True)
    root = lax.rsqrt(jnp.mean(centred * centred, axis=-1, keepdims=True) + 1e-05)
    return centred * root, root


def turn(m, c, s1, s2):
    return m * c + pltpu.roll(m, 120, 1) * s1 + pltpu.roll(m, 8, 1) * s2


def kv_tables(c, s1, s2):
    key = lax.broadcasted_iota(jnp.int32, c.shape, 1) < 64
    return jnp.where(key, c, 1.0), jnp.where(key, s1, 0.0), jnp.where(key, s2, 0.0)


def front_kernel(ids, x, p_own, pu, c, s1, s2, first, kv, p_copy, up0):
    p_oth = pu.at[: p_own.shape[0]]
    p_copy[...] = p_oth[...]
    for k in range(3):
        up0[:, k * 128 : (k + 1) * 128] = pu[416 + 384 * k : 800 + 384 * k, :]
    side = ids[1]
    half = x.shape[1] // 2
    own, other = p_own[half:].astype(f32), p_oth[half:].astype(f32)
    hat, _ = normalize(x[...].astype(f32))
    first[...] = (hat * model_vector(side, own, other, 0) + model_vector(side, own, other, 1)).astype(bf16)
    m = mm(first[:, lanes(side * half, half)], p_own[:half])
    m += mm(first[:, lanes((1 - side) * half, half)], p_oth[:half])
    m += qkv_bias_tiles(side, own, other)[6]
    kv[...] = turn(m, *kv_tables(c[...], s1[...], s2[...])).astype(bf16)


def query_kernel(ids, first, w, w_mine, w_theirs, p_own, p_oth, c, s1, s2, q, w_copy, bias):
    side, core = ids[1], ids[2]
    half = first.shape[1] // 2
    tiles = qkv_bias_tiles(side, p_own[half:].astype(f32), p_oth[half:].astype(f32))
    bias[...] = jnp.concatenate(tiles[:6], axis=1)
    for ref, cb in ((w_mine, core), (w_theirs, 1 - core)):
        col = cb * half
        w_copy[:, lanes(col, half)] = ref[...]
        m = mm(first[:, lanes(side * half, half)], w[:, lanes(col, half)])
        m += mm(first[:, lanes((1 - side) * half, half)], ref[...])
        m += bias[:, lanes(col, half)]
        for k in range(half // 128):
            low = turn(m[:, k * 128 : (k + 1) * 128], c[...], s1[...], s2[...]).astype(bf16)
            q[:, lanes(col + k * 128, 128)] = (low.astype(f32) * 0.125).astype(bf16)


def cotangent_kernel(dy_own, xd, w, g_own, g_oth, q_mine):
    rows = q_mine.shape[0] // 2
    q_mine[:rows] = xd[2 * dy_own.shape[0] :, : 2 * rows]
    q_mine[rows:] = xd[2 * dy_own.shape[0] :, 2 * rows :]
    g_own[...] = mm(dy_own[...], w[...], NT).astype(bf16)
    g_oth[...] = mm(xd[dy_own.shape[0] : 2 * dy_own.shape[0]], w[...], NT).astype(bf16)


def ff_kernel(
    ids, x_own, xd, dy_own, up, up0, up1, up2, up3, down, up_bias, p_own, p_oth,
    keep_a, send_a, keep_b, send_b, act, dh, hat_oth, first_oth, hat_half, dy_copy, up_sum,
    a2, dy, bias, g_down, g_up, up_buf, down_buf, up_sem, down_sem,
):
    side, core, near_y = ids[1], ids[2], ids[3]
    tokens, width = x_own.shape
    x_oth, dy_oth = xd.at[:tokens], xd.at[tokens : 2 * tokens]
    half = width // 2
    wide = act.shape[1]
    step = wide // 4
    pieces = [
        (ref, (jnp.bitwise_xor(core, a) * 2 + jnp.bitwise_xor(near_y, b)), a, b)
        for ref, a, b in ((up0, 0, 0), (up1, 0, 1), (up2, 1, 0), (up3, 1, 1))
    ]

    def up_copy(i, piece):
        at = lanes(side * wide + piece * step, step)
        return pltpu.make_async_copy(up.at[:, at], up_buf.at[i], up_sem.at[i])

    def down_copy(i, piece):
        at = pl.ds(pl.multiple_of(piece * step, step), step)
        return pltpu.make_async_copy(down.at[at, :], down_buf.at[i], down_sem.at[i])

    for i, (_, piece, _, _) in enumerate(pieces):
        up_copy(i, piece).start()
        down_copy(i, piece).start()
    own, other = p_own[half:].astype(f32), p_oth[half:].astype(f32)
    gain1, shift1 = model_vector(side, own, other, 0), model_vector(side, own, other, 1)
    gain2, shift2 = model_vector(side, own, other, 2), model_vector(side, own, other, 3)
    mine, theirs = lanes(side * half, half), lanes((1 - side) * half, half)
    hat_own, _ = normalize(x_own[...].astype(f32))
    a2[:tokens] = (hat_own * gain2 + shift2).astype(bf16)
    hat_other, _ = normalize(x_oth[...].astype(f32))
    hat_oth[...] = hat_other
    a2[tokens:] = (hat_other * gain2 + shift2).astype(bf16)
    first_oth[...] = (hat_other * gain1 + shift1).astype(bf16)
    hat_half[...] = jnp.where(side == 0, hat_other[:, :half], hat_other[:, half:])
    dy[:tokens] = dy_own[...]
    dy[tokens:] = dy_oth[...]
    dy_copy[...] = dy_oth[...]
    bias[...] = up_bias[...].astype(f32).reshape(1, wide)
    rows = half // 4
    far = ids[0] // 4 % 4
    for i, (ref, piece, a, b) in enumerate(pieces):
        up_copy(i, piece).wait()
        down_copy(i, piece).wait()
        cols = lanes(piece * step, step)
        h = mm(a2[:, mine], up_buf[i])
        h += mm(a2[:, theirs], ref[...])
        h += bias[:, cols]
        phi = 0.5 * (1.0 + lax.erf(h * 0.7071067811865476))
        slope = phi + h * jnp.exp(-0.5 * h * h) * 0.3989422804014327
        g = (h * phi).astype(bf16)
        act[:, i * step : (i + 1) * step] = g
        d = mm(dy[...], down_buf[i], NT)
        e = (d * slope).astype(bf16)
        dh[:, i * step : (i + 1) * step] = e
        up_sum[:, cols] = jnp.sum(e.astype(f32), axis=0, keepdims=True)
        g_down[...] = mm(g, dy[...], TN).astype(bf16)
        g_up[:, :half] = mm(a2[:, mine], e, TN).astype(bf16)
        g_up[:, half:] = mm(a2[:, theirs], e, TN).astype(bf16)
        for k in range(4):
            z = jnp.bitwise_xor(far, (k & 1) * 2 + (k >> 1))
            at = pl.ds(pl.multiple_of(z * rows, rows), rows)
            slot = b * 4 + k
            (send_a if a else keep_a)[slot] = g_down[at, :]
            (send_b if a else keep_b)[slot] = g_up[at, :]


def ff_rest_kernel(
    ids, act, dh, x_own, hat_oth, up, up0, up1, up2, up3, down,
    ff_own, ff_oth, ds_own, ds_oth, n_mine, n_send, sums, up_buf, down_buf, up_sem, down_sem,
):
    side, core, near_y = ids[1], ids[2], ids[3]
    tokens, width = x_own.shape
    half = width // 2
    wide = act.shape[1]
    step = wide // 4
    order = ((0, 0), (0, 1), (1, 0), (1, 1))
    pieces = [jnp.bitwise_xor(core, a) * 2 + jnp.bitwise_xor(near_y, b) for a, b in order]
    copies = []
    for i, piece in enumerate(pieces):
        at = pl.ds(pl.multiple_of(piece * step, step), step)
        copies.append(pltpu.make_async_copy(down.at[at, :], down_buf.at[i], down_sem.at[i]))
        at = lanes(side * wide + piece * step, step)
        copies.append(pltpu.make_async_copy(up.at[:, at], up_buf.at[i], up_sem.at[i]))
    for copy in copies:
        copy.start()
    hat_own, _ = normalize(x_own[...].astype(f32))
    for copy in copies:
        copy.wait()
    out = sum(mm(act[:, i * step : (i + 1) * step], down_buf[i]) for i in range(4))
    ff_own[...] = out[:tokens]
    ff_oth[...] = out[tokens:]
    ds_mine = sum(mm(dh[:, i * step : (i + 1) * step], up_buf[i], NT) for i in range(4))
    ds_theirs = sum(
        mm(dh[:, i * step : (i + 1) * step], ref[...], NT) for i, ref in enumerate((up0, up1, up2, up3))
    )
    low = jnp.where(side == 0, ds_mine, ds_theirs)
    high = jnp.where(side == 0, ds_theirs, ds_mine)
    for part, ds in ((slice(0, half), low), (slice(half, width), high)):
        ds_own[:, part] = ds[:tokens]
        ds_oth[:, part] = ds[tokens:].astype(bf16)
        moved = ds[:tokens] * hat_own[:, part] + ds[tokens:] * hat_oth[:, part]
        sums[0:1, part] = jnp.sum(moved, axis=0, keepdims=True)
        sums[1:2, part] = jnp.sum(ds, axis=0, keepdims=True)
    split_rows(sums, 2, side, half, n_mine, n_send)


def split_rows(sums, count, side, half, mine, send):
    for ref, owner in ((mine, side), (send, 1 - side)):
        ref[...] = jnp.zeros_like(ref)
        for i in range(count):
            for k in range(half // 128):
                at = i * (half // 128) + k
                ref[at : at + 1, :] = sums[i : i + 1, lanes(owner * half + k * 128, 128)]


class Block:
    def __init__(self, stages, n_dev, docs, side, ids, len_ref):
        self.stages, self.n_dev, self.me, self.fsdp = stages, n_dev, ids[0], ids[1]
        self.block = ids[0] if side == 0 else 2 * n_dev - 1 - ids[0]
        self.rows = pl.ds(side * BLOCK, BLOCK)
        self.low = lax.broadcasted_iota(jnp.int32, (BLOCK, 128), 1) < 64
        base = self.block * BLOCK
        self.qpos = base + lax.broadcasted_iota(jnp.int32, (1, BLOCK), 1)
        total = first = jnp.int32(0)
        self.qstart = jnp.zeros((1, BLOCK), jnp.int32)
        for e in range(docs):
            size = len_ref[0, e]
            total = total + size
            self.qstart = self.qstart + jnp.where(total <= self.qpos, size, 0)
            first = first + jnp.where(total <= base, size, 0)
        self.steps = (base + BLOCK - first + 2 * BLOCK - 1) // (2 * BLOCK)

    def row_of(self, j):
        j = jnp.maximum(j, 0)
        dev = jnp.where(j < self.n_dev, j, 2 * self.n_dev - 1 - j)
        slot = slot_of(jnp.bitwise_xor(dev, self.me), self.stages)
        return pl.multiple_of((slot * 2 + jnp.where(j < self.n_dev, 0, 1)) * BLOCK, BLOCK)

    def columns(self, p, half):
        close = p < half // 128
        local = (p % (half // 128)) * 128
        return close, local, lanes((self.fsdp if close else 1 - self.fsdp) * half + local, 128)

    def half_turn(self, two):
        return pltpu.roll(two.astype(f32), 64, 1).astype(bf16)

    def spread_query(self, q_ref, qz):
        for p in range(q_ref.shape[1] // 128):
            two = q_ref[self.rows, self.columns(p, q_ref.shape[1] // 2)[2]]
            zero = jnp.zeros_like(two)
            qz[pl.ds(p * 256, 128), :] = jnp.where(self.low, two, zero)
            qz[pl.ds(p * 256 + 128, 128), :] = jnp.where(self.low, self.half_turn(two), zero)

    def load(self, t, kv_mine, kv_theirs, bias):
        middle = kv_mine.shape[0]
        parts, at = [], []
        hi = self.block - 2 * t
        for j in (hi - 1, hi):
            row = self.row_of(j)
            inner = pl.multiple_of(jnp.where(row < middle, row, row - middle), BLOCK)
            here = pl.ds(inner, BLOCK)
            parts.append(jnp.where(row < middle, kv_mine[here, :], kv_theirs[here, :]))
            at.append(row)
        kpos = (hi - 1) * BLOCK + lax.broadcasted_iota(jnp.int32, (2 * BLOCK, BLOCK), 0)
        ok = (kpos <= self.qpos) & (kpos >= self.qstart)
        bias[...] = jnp.where(ok, 0.0, -1e30)
        return jnp.concatenate(parts, axis=0), at


def attn_forward_kernel(
    stages, n_dev, docs, side, ids, len_ref, q_ref, kv_mine, kv_theirs, g_own, g_oth,
    o_own, o_oth, st, qz, ot, bias,
):
    me = Block(stages, n_dev, docs, side, ids, len_ref)
    half = q_ref.shape[1] // 2
    pairs = q_ref.shape[1] // 128
    me.spread_query(q_ref, qz)
    ot[...] = jnp.zeros_like(ot)
    st[0] = jnp.full(st.shape[1:], -1e30, f32)
    st[1] = jnp.zeros(st.shape[1:], f32)

    def forward(t, carry):
        kvb, _ = me.load(t, kv_mine, kv_theirs, bias)
        vt = kvb.astype(f32).T.astype(bf16)[64:]
        mask = bias[...]
        for p in range(pairs):
            s2 = mm(kvb, qz[pl.ds(p * 256, 256), :], NT)
            for i in range(2):
                h = 2 * p + i
                s = s2[:, i * 128 : (i + 1) * 128] + mask
                old = st[0, h : h + 1, :]
                new = jnp.maximum(old, jnp.max(s, axis=0, keepdims=True))
                e = jnp.exp(s - new)
                alpha = jnp.exp(old - new)
                st[0, h : h + 1, :] = new
                st[1, h : h + 1, :] = st[1, h : h + 1, :] * alpha + jnp.sum(e, axis=0, keepdims=True)
                hs = pl.ds(h * 64, 64)
                ot[hs, :] = ot[hs, :] * alpha + mm(vt, e.astype(bf16))
        return 0

    lax.fori_loop(0, me.steps, forward, 0)
    for p in range(pairs):
        close, local, _ = me.columns(p, half)
        gt = (g_own if close else g_oth)[me.rows, pl.ds(local, 128)].astype(f32).T
        halves = []
        for i in range(2):
            h = 2 * p + i
            l = st[1, h : h + 1, :]
            o = ot[pl.ds(h * 64, 64), :] / l
            halves.append(o)
            st[2, h : h + 1, :] = jnp.sum(o * gt[i * 64 : (i + 1) * 64], axis=0, keepdims=True)
            st[0, h : h + 1, :] = st[0, h : h + 1, :] + jnp.log(l)
        (o_own if close else o_oth)[:, pl.ds(local, 128)] = jnp.concatenate(halves, axis=0).T.astype(bf16)


def attn_backward_kernel(stages, n_dev, docs, side, last, *refs):
    ids, len_ref, q_ref, kv_mine, kv_theirs, g_own, g_oth, st, cos_ref, sin_ref = refs[:10]
    if not last:
        dm_ref, acc, qz, gz, dqt, bias, ds_sc, p_sc = refs[10:]
        acc[...] = jnp.zeros_like(acc)
    else:
        before, dm_ref, dkv_keep, dkv_send, qz, gz, dqt, bias, ds_sc, p_sc, acc = refs[10:]
        acc[...] = before[...]
    me = Block(stages, n_dev, docs, side, ids, len_ref)
    half = q_ref.shape[1] // 2
    pairs = q_ref.shape[1] // 128
    me.spread_query(q_ref, qz)
    for p in range(pairs):
        close, local, _ = me.columns(p, half)
        two = (g_own if close else g_oth)[me.rows, pl.ds(local, 128)]
        zero = jnp.zeros_like(two)
        gz[pl.ds(p * 256, 128), :] = jnp.where(me.low, zero, me.half_turn(two))
        gz[pl.ds(p * 256 + 128, 128), :] = jnp.where(me.low, zero, two)
    dqt[...] = jnp.zeros_like(dqt)

    def backward(t, carry):
        kvb, at = me.load(t, kv_mine, kv_theirs, bias)
        kt = kvb.astype(f32).T.astype(bf16)[:64]
        mask = bias[...]
        for p in range(pairs):
            s2 = mm(kvb, qz[pl.ds(p * 256, 256), :], NT)
            dp2 = mm(kvb, gz[pl.ds(p * 256, 256), :], NT)
            for i in range(2):
                h = 2 * p + i
                sl = slice(i * 128, (i + 1) * 128)
                pr = jnp.exp((s2[:, sl] + mask) - st[0, h : h + 1, :])
                ds = pr * (dp2[:, sl] - st[2, h : h + 1, :])
                ds_sc[:, h * 128 : (h + 1) * 128] = ds.astype(bf16)
                p_sc[:, h * 128 : (h + 1) * 128] = pr.astype(bf16)
        part = mm(ds_sc[...], qz[...]) + mm(p_sc[...], gz[...])
        for i in range(2):
            acc[pl.ds(at[i], BLOCK), :] += part[i * BLOCK : (i + 1) * BLOCK]
        dqt[...] += mm(kt, ds_sc[...])
        return 0

    lax.fori_loop(0, me.steps, backward, 0)
    cos = cos_ref[side]
    sin = sin_ref[side]
    for p in range(pairs):
        halves = []
        for i in range(2):
            h = 2 * p + i
            g = dqt[:, h * 128 : (h + 1) * 128] * 0.125
            g0, g1 = g[:8], g[8:16]
            halves += [g0 * cos + g1 * sin, g1 * cos - g0 * sin, g[16:]]
        dm_ref[:, me.columns(p, half)[2]] = jnp.concatenate(halves, axis=0).T.astype(bf16)
    if last:
        middle = dkv_keep.shape[0]
        dkv_keep[...] = acc[:middle].astype(bf16)
        dkv_send[...] = acc[middle:].astype(bf16)


def attn_forward(side, stages, n_dev, ids, lengths, q, kv, g_own, g_oth):
    width = q.shape[1]
    block = q.shape[0] // 2
    rows = width // 64 * 128
    kv = near(*kv) if n_dev <= LOW else kv
    return call(
        partial(attn_forward_kernel, stages, n_dev, lengths.shape[1], side),
        "attn_forward",
        [((block, width // 2), bf16, False), ((block, width // 2), bf16, True), ((3, 16, 128), f32, True)],
        (ids, lengths, *near(q), *kv, g_own, *near(g_oth)),
        scratch=[pltpu.VMEM((rows, 128), bf16), pltpu.VMEM((width, 128), f32), pltpu.VMEM((256, 128), f32)],
        room=6 + (0 if n_dev <= LOW else kv[0].size * 4 // 2**20),
    )


def attn_backward(side, stages, n_dev, ids, lengths, q, kv, g_own, g_oth, st, cos, sin, before=()):
    width = q.shape[1]
    block = q.shape[0] // 2
    middle = kv[0].shape[0]
    rows = width // 64 * 128
    small = n_dev <= LOW
    close = near if small else (lambda *values: values)
    outs = [((block, width), bf16, True)]
    last = len(before) > 0
    outs += [((middle, 128), bf16, True)] * 2 if last else [((2 * middle, 128), f32, small)]
    scratch = [
        pltpu.VMEM((rows, 128), bf16),
        pltpu.VMEM((rows, 128), bf16),
        pltpu.VMEM((64, rows), f32),
        pltpu.VMEM((256, 128), f32),
        pltpu.VMEM((256, rows), bf16),
        pltpu.VMEM((256, rows), bf16),
    ]
    if last:
        scratch += [pltpu.VMEM((2 * middle, 128), f32)]
    return call(
        partial(attn_backward_kernel, stages, n_dev, lengths.shape[1], side, last),
        "attn_backward",
        outs,
        (ids, lengths, *near(q), *close(*kv), g_own, *near(g_oth, st), cos, sin, *close(*before)),
        scratch=scratch,
        room=8 + 2 * middle * 128 * (4 if small else 7) // 2**20,
    )


def pile_kernel(a0, a1, b0, b1, c0, c1, *outs):
    for out, parts in zip(outs, ((a0, a1), (b0, b1), (c0, c1))):
        rows = parts[0].shape[0]
        out[:rows] = parts[0][...]
        out[rows:] = parts[1][...]


def mix_kernel(ff, o, w, out):
    out[...] = (ff[...] + mm(o[...], w[...])).astype(bf16)


def result_kernel(ids, x, ff, o, w, recv, p_own, p_oth, out):
    side = ids[1]
    half = x.shape[1] // 2
    own, other = p_own[half:].astype(f32), p_oth[half:].astype(f32)
    y = x[...].astype(f32) + (ff[...] + mm(o[...], w[...])) + recv[...].astype(f32)
    y += model_vector(side, own, other, 4) + model_vector(side, own, other, 5)
    out[...] = y.astype(bf16)


def dm_kv_kernel(*refs):
    later, c, s1, s2, out = refs[-5:]
    total = later[...]
    for ref in refs[:-5]:
        total = total + ref[...].astype(f32)
    c, s1, s2 = kv_tables(c[...], s1[...], s2[...])
    out[...] = turn(total, c, -s1, -s2).astype(bf16)


def x_grad_kernel(ids, x, dy, dm, dm_kv, w, w_oth, p_own, p_oth, ds, ds_recv, out, da):
    side = ids[1]
    width = x.shape[1]
    half = width // 2
    own, other = p_own[half:].astype(f32), p_oth[half:].astype(f32)
    mine, theirs = lanes(side * half, half), lanes((1 - side) * half, half)
    da[:, mine] = mm(dm[...], w[:, :width], NT) + mm(dm_kv[...], p_own[:half], NT)
    da[:, theirs] = mm(dm[...], w_oth[...], NT) + mm(dm_kv[...], p_oth[:half], NT)
    hat, root = normalize(x[...].astype(f32))
    total = dy[...].astype(f32)
    for i, grad in enumerate((da[...], ds[...] + ds_recv[...].astype(f32))):
        up = grad * model_vector(side, own, other, 2 * i)
        total += root * (
            up - jnp.mean(up, axis=-1, keepdims=True) - hat * jnp.mean(up * hat, axis=-1, keepdims=True)
        )
    out[...] = total


def pair_kernel(ids, f_own, f_oth, dm_own, dm_oth, o_own, o_oth, dy_own, dy_oth, keep, send, gq, go):
    side, core = ids[1], ids[2]
    half = f_own.shape[1] // 2
    mine = lanes(side * half, half)
    gq[...] = mm(f_own[:, mine], dm_own[...], TN) + mm(f_oth[:, mine], dm_oth[...], TN)
    go[...] = mm(o_own[...], dy_own[...], TN) + mm(o_oth[...], dy_oth[...], TN)
    rows = half // 8
    close = ids[0] % LOW // 2
    for ref, cb in ((keep, core), (send, 1 - core)):
        cols = lanes(cb * half, half)
        for k in range(8):
            at = pl.ds(pl.multiple_of(jnp.bitwise_xor(close, CHUNKS[k]) * rows, rows), rows)
            ref[k * rows : (k + 1) * rows, 0:half] = gq[at, cols].astype(bf16)
            ref[k * rows : (k + 1) * rows, half:] = go[at, cols].astype(bf16)


def tail_kernel(
    ids, f_own, f_oth, dm_own, dm_oth, dy_own, dy_oth, kv_own, kv_oth, n_mine, n_recv, up_sum,
    x_own, hat_half, w, p_own, out, tail, hat,
):
    side = ids[1]
    half = f_own.shape[1] // 2
    mine = lanes(side * half, half)
    tail[:half] = mm(f_own[:, mine], kv_own[...], TN) + mm(f_oth[:, mine], kv_oth[...], TN)
    tail[half:] = jnp.zeros((32, 128), f32)
    gain = shift = 0.0
    hat[...] = normalize(x_own[...].astype(f32))[0]
    for x, dm, kv in ((hat[:, mine], dm_own, kv_own), (hat_half[...], dm_oth, kv_oth)):
        grad = mm(dm[...], w[:, : 2 * half], NT) + mm(kv[...], p_own[:half], NT)
        gain += jnp.sum(grad * x, axis=0, keepdims=True)
        shift += jnp.sum(grad, axis=0, keepdims=True)
    row = half
    for v in (gain, shift):
        for k in range(3):
            tail[row + k : row + k + 1, :] = v[:, k * 128 : (k + 1) * 128]
        row += 3
    v = n_mine[...] + n_recv[...]
    tail[row : row + 6] = v[:6]
    row += 6

    def total(a, b):
        return jnp.sum(a.astype(f32), axis=0, keepdims=True) + jnp.sum(b.astype(f32), axis=0, keepdims=True)

    v = total(dy_own[:, mine], dy_oth[:, mine])
    for k in range(3):
        tail[row + k : row + k + 1, :] = v[:, k * 128 : (k + 1) * 128]
    row += 3
    v = jnp.concatenate([total(dm_own[...], dm_oth[...]), total(kv_own[...], kv_oth[...])], axis=1)
    moved = jnp.concatenate([v[:, 448:], v[:, :448]], axis=1)
    v = jnp.where(side == 0, v, moved)
    for k in range(4):
        tail[row + k : row + k + 1, :] = v[:, k * 128 : (k + 1) * 128]
    row += 4
    for k in range(12):
        tail[row + k : row + k + 1, :] = up_sum[:, k * 128 : (k + 1) * 128]
    out[...] = tail[...].astype(bf16)


def sum_kernel(*refs):
    total = refs[0][...].astype(f32)
    for ref in refs[1:-1]:
        total = total + ref[...].astype(f32)
    refs[-1][...] = total.astype(refs[-1].dtype)


def sum_of(first, second, name):
    return call(sum_kernel, name, [(first.shape, first.dtype, True)], near(first, second))[0]


def up_part_kernel(a, b, own, other):
    half = own.shape[-1]
    total = a[...].astype(f32) + b[...].astype(f32)
    own[...] = total[..., :half].astype(bf16)
    other[...] = total[..., half:].astype(bf16)


def up_join_kernel(own, other, out):
    half = own.shape[-1]
    out[..., :half] = own[...]
    out[..., half:] = other[...]


def chunk_of(ids, other_core, slot):
    core, near_y, far = ids[2], ids[3], ids[0] // 4 % 4
    piece = jnp.bitwise_xor(core, other_core) * 2 + jnp.bitwise_xor(near_y, slot >> 2)
    return piece, jnp.bitwise_xor(far, (slot & 1) * 2 + (slot >> 1 & 1))


def down_out_kernel(ids, mine, theirs, out):
    rows = mine.shape[1]
    for a, ref in enumerate((mine, theirs)):
        for k in range(8):
            piece, z = chunk_of(ids, a, k)
            out[pl.ds(pl.multiple_of((piece * 4 + z) * rows, rows), rows), :] = ref[k].astype(f32)


def up_out_kernel(ids, mine, theirs, out):
    side = ids[1]
    rows = mine.shape[1]
    half = mine.shape[2] // 2
    wide = out.shape[1] // 2
    for a, ref in enumerate((mine, theirs)):
        for k in range(8):
            piece, z = chunk_of(ids, a, k)
            at = pl.ds(pl.multiple_of(z * rows, rows), rows)
            for j, owner in ((0, side), (1, 1 - side)):
                part = ref[k, :, j * half : (j + 1) * half].astype(f32)
                out[at, lanes(owner * wide + piece * half, half)] = part


def attn_out_kernel(ids, p_mine, p_theirs, tail, g_qkv, g_out, n0, n1, n2, n3, qb, ob, ub, db):
    core = ids[2]
    close = ids[0] % LOW // 2
    half = g_qkv.shape[0]
    rows = half // 8
    for ref, cb in ((p_mine, core), (p_theirs, 1 - core)):
        cols = lanes(cb * half, half)
        for k in range(8):
            at = pl.ds(pl.multiple_of(jnp.bitwise_xor(close, CHUNKS[k]) * rows, rows), rows)
            part = ref[k * rows : (k + 1) * rows, :].astype(f32)
            g_qkv[at, cols] = part[:, :half]
            g_out[at, cols] = part[:, half:]
    g_qkv[:, 2 * half :] = tail[:half].astype(f32)
    small = tail[half:].astype(f32)
    for i, ref in enumerate((n0, n1, n2, n3, ob)):
        ref[...] = row_vector(small, 3 * i).reshape(half)
    db[...] = row_vector(small, 12).reshape(half)
    qb[...] = row_vector(small, 15, 4)[:, : qb.shape[0]].reshape(qb.shape[0])
    ub[...] = row_vector(small, 19, 12).reshape(ub.shape[0])


def body(
    layer_input, doc_lengths, ln1_gain, ln1_bias, ln2_gain, ln2_bias, qkv_weight, qkv_bias,
    out_weight, out_bias, up_weight, up_bias, down_weight, down_bias, out_grad, kv_grad_later,
):
    devices = lax.axis_size("ctx")
    me = lax.axis_index("ctx").astype(jnp.int32)
    side = lax.axis_index("fsdp").astype(jnp.int32)
    ids = jnp.stack([me, side, me % 2, me // 2 % 2])
    tokens, width = layer_input.shape[1:]
    half_rows = tokens // 2
    half = width // 2
    wide = up_weight.shape[1] // 2
    stages = stages_of(devices)
    x_own, dy_own = layer_input[0], out_grad[0]

    vectors = (ln1_gain, ln1_bias, ln2_gain, ln2_bias, out_bias, down_bias, qkv_bias)
    p_own, pu_own, xd_own = pack(ids, x_own, dy_own, qkv_weight, up_weight, vectors)
    pu_oth = swap_x(pu_own)
    xd = swap_x(after(xd_own, pu_oth))

    offsets = jnp.arange(half_rows, dtype=jnp.int32)
    places = jnp.concatenate([me * half_rows + offsets, (2 * devices - 1 - me) * half_rows + offsets]).astype(f32)
    half_rot = ROT // 2
    freq = 10000.0 ** (-jnp.arange(half_rot, dtype=f32) / half_rot)
    lane = np.arange(128)
    angles = places[:, None] * jnp.tile(freq, 128 // half_rot)[None, :]
    cosine, sine = jnp.cos(angles), jnp.sin(angles)
    tables = (
        jnp.where(lane % 64 < 16, cosine, 1.0),
        jnp.where(lane % 64 < 8, -sine, 0.0),
        jnp.where((lane % 64 >= 8) & (lane % 64 < 16), sine, 0.0),
    )
    t_angles = places.reshape(2, 1, half_rows) * freq[None, :, None]
    cos_t, sin_t = jnp.cos(t_angles), jnp.sin(t_angles)

    first_own, kv, p_oth, up0 = call(
        front_kernel,
        "front",
        [
            ((tokens, width), bf16, False), ((tokens, 128), bf16, True), (p_own.shape, bf16, False),
            ((half, half), bf16, True),
        ],
        (ids, x_own, p_own, *near(pu_oth), *tables),
    )
    up1, up2 = swap_ctx(up0, 2), swap_ctx(up0, 1)
    kv = gather_step(kv, stages[0][0], "kv_join")
    ups = (up0, up1, up2, swap_ctx(after(up1, kv), 1))
    for stride, _ in stages[1:-2]:
        kv = gather_step(kv, stride, "kv_join")
    kv_mine = gather_step(kv, 2, "kv_join")
    kv_theirs = swap_ctx(kv_mine, 1)

    g_own, g_send, q_mine = call(
        cotangent_kernel,
        "cotangent",
        [((tokens, half), bf16, False), ((tokens, half), bf16, True), ((half, half), bf16, True)],
        (dy_own, *near(xd), out_weight),
    )
    g_oth = swap_x(g_send)
    q_theirs = swap_ctx(q_mine, 1)

    rows = half // 4
    step = wide // 4
    chunks = ((8, rows, width), bf16, True)
    token_f32, token_low = ((tokens, width), f32, False), ((tokens, width), bf16, False)
    (
        keep_a, send_a, keep_b, send_b, act, dh, hat_oth, first_oth, hat_half, dy_far, up_sum,
    ) = call(
        ff_kernel,
        "ff",
        [
            chunks, chunks, chunks, chunks, ((2 * tokens, wide), bf16, True), ((2 * tokens, wide), bf16, True),
            token_f32, token_low, ((tokens, half), f32, False), token_low, ((1, wide), f32, False),
        ],
        (
            ids, x_own, *near(after(xd, kv_mine, g_send)), dy_own, Raw(up_weight), *near(*ups), Raw(down_weight),
            up_bias, p_own, p_oth,
        ),
        scratch=[
            pltpu.VMEM((2 * tokens, width), bf16),
            pltpu.VMEM((2 * tokens, width), bf16),
            pltpu.VMEM((1, wide), f32),
            pltpu.VMEM((half, width), bf16),
            pltpu.VMEM((half, width), bf16),
            pltpu.VMEM((4, half, step), bf16),
            pltpu.VMEM((4, step, width), bf16),
            pltpu.SemaphoreType.DMA((4,)),
            pltpu.SemaphoreType.DMA((4,)),
        ],
        room=16,
    )
    row_block = ((8, 128), f32, False)
    ff_own, ff_oth, ds_own, ds_oth, n_mine, n_send = call(
        ff_rest_kernel,
        "ff_rest",
        [token_f32, token_f32, token_f32, token_low, row_block, row_block],
        (ids, *near(act, dh), x_own, hat_oth, Raw(up_weight), *near(*ups), Raw(down_weight)),
        scratch=[
            pltpu.VMEM((8, width), f32),
            pltpu.VMEM((4, half, step), bf16),
            pltpu.VMEM((4, step, width), bf16),
            pltpu.SemaphoreType.DMA((4,)),
            pltpu.SemaphoreType.DMA((4,)),
        ],
        room=18,
    )
    n_recv = swap_x(n_send)
    ds_recv = swap_x(ds_oth)
    low = min(LOW, devices)
    keep_a, send_a = scatter_step(keep_a, send_a, 1, "down_add")
    keep_b, send_b = scatter_step(keep_b, send_b, 1, "up_add")
    q, q_far = call(
        query_kernel,
        "query",
        [((tokens, width), bf16, True), ((half, width), bf16, False)],
        (ids, first_own, qkv_weight, *near(q_mine, q_theirs), p_own, p_oth, *tables),
        scratch=[pltpu.VMEM((1, width), f32)],
    )
    pairs = (stages, devices, ids, doc_lengths)
    q = after(q, send_a, send_b)
    kv_all = (kv_mine, kv_theirs)
    o_own0, o_send0, st0 = attn_forward(0, *pairs, q, kv_all, g_own, g_oth)
    keep_a, send_a = scatter_step(after(keep_a, st0), send_a, 2, "down_add")
    dm_own0, dkv = attn_backward(0, *pairs, after(q, send_a), kv_all, g_own, g_oth, st0, cos_t, sin_t)
    keep_b, send_b = scatter_step(after(keep_b, dm_own0), send_b, 2, "up_add")
    o_own1, o_send1, st1 = attn_forward(1, *pairs, after(q, send_b), kv_all, g_own, g_oth)
    keep_a, send_a = scatter_step(after(keep_a, st1), send_a, 4, "down_add")
    if devices <= LOW:
        dm_own1, dkv_keep, dkv_send = attn_backward(
            1, *pairs, after(q, send_a), kv_all, g_own, g_oth, st1, cos_t, sin_t, before=(dkv,)
        )
    else:
        dm_own1, dkv_more = attn_backward(1, *pairs, after(q, send_a), kv_all, g_own, g_oth, st1, cos_t, sin_t)
        dkv = (dkv + dkv_more).astype(bf16)
        dkv_keep, dkv_send = dkv[: kv_mine.shape[0]], dkv[kv_mine.shape[0] :]
    keep_b, send_b = scatter_step(after(keep_b, dm_own1), send_b, 4, "up_add")
    down_part = high_sum(sum_of(*scatter(keep_a, send_a, low, "down_add", 8), "down_sum"))
    up_own, up_send = call(
        up_part_kernel,
        "up_part",
        [((1, rows, half), bf16, True), ((1, rows, half), bf16, True)],
        near(*scatter(keep_b, send_b, low, "up_add", 8)),
    )
    up_own, up_send = high_sum(up_own), high_sum(up_send)
    up_part = call(up_join_kernel, "up_join", [((1, rows, width), bf16, True)], near(up_own, swap_x(up_send)))[0]
    o_own, o_send, dm_own = call(
        pile_kernel,
        "pile",
        [((tokens, half), bf16, False), ((tokens, half), bf16, True), ((tokens, width), bf16, True)],
        (o_own0, o_own1, *near(o_send0, o_send1, dm_own0, dm_own1)),
    )
    kv_pieces = scatter(dkv_keep, dkv_send, devices, "kv_add")
    o_oth = swap_x(o_send)
    dm_oth = swap_x(dm_own)

    y_send = call(mix_kernel, "mix", [((tokens, width), bf16, True)], (ff_oth, *near(o_oth), out_weight))[0]
    y_recv = swap_x(y_send)
    result = call(
        result_kernel,
        "result",
        [((tokens, width), bf16, False)],
        (ids, x_own, ff_own, o_own, out_weight, *near(y_recv), p_own, p_oth),
    )[0]

    kv_pieces = (after(kv_pieces[0], ds_recv), kv_pieces[1])
    dm_kv = call(
        dm_kv_kernel, "dm_kv", [((tokens, 128), bf16, True)], (*near(*kv_pieces), kv_grad_later[0], *tables)
    )[0]
    dm_kv_oth = swap_x(dm_kv)
    grad_inputs = call(
        x_grad_kernel,
        "x_grad",
        [((tokens, width), f32, False)],
        (
            ids, x_own, dy_own, *near(dm_own, dm_kv), qkv_weight, q_far, p_own, p_oth, ds_own,
            *near(ds_recv),
        ),
        scratch=[pltpu.VMEM((tokens, width), f32)],
        room=8,
    )[0]
    keep, send = call(
        pair_kernel,
        "pair",
        [((half, width), bf16, True), ((half, width), bf16, True)],
        (ids, first_own, first_oth, *near(dm_own, dm_oth), o_own, *near(o_oth), dy_own, dy_far),
        scratch=[pltpu.VMEM((half, width), f32), pltpu.VMEM((half, width), f32)],
        room=8,
    )
    pieces = scatter(keep, send, low, "pair_add")
    pair = high_sum(sum_of(pieces[0], pieces[1], "pair_sum"))
    tail = call(
        tail_kernel,
        "tail",
        [((half + 32, 128), bf16, True)],
        (
            ids, first_own, first_oth, *near(dm_own, dm_oth), dy_own, dy_far, *near(dm_kv, dm_kv_oth), n_mine,
            *near(n_recv), up_sum, x_own, hat_half, qkv_weight, p_own,
        ),
        scratch=[pltpu.VMEM((half + 32, 128), f32), pltpu.VMEM((tokens, width), f32)],
        room=8,
    )[0]
    outs = []
    for value, name in ((down_part, "down_join"), (up_part, "up_join"), (pair, "pair_join")):
        for stride, _ in stages_of(low)[:-1]:
            value = gather_step(value, stride, name)
        outs.append(near(value, swap_ctx(value, 1)))
    g_down = call(down_out_kernel, "down_out", [((wide, width), f32, False)], (ids, *outs[0]), room=8)[0]
    g_up = call(up_out_kernel, "up_out", [((half, 2 * wide), f32, False)], (ids, *outs[1]), room=8)[0]
    for i, (stride, _) in enumerate(stages[::-1]):
        other = swap_ctx(tail, stride)
        if i == 2:
            tail = after(tail, result, grad_inputs)
        if i == 3:
            tail = after(tail, g_down, g_up)
        tail = sum_of(tail, other, "tail_sum")
    vec = ((half,), f32, False)
    g_qkv, g_out, *small = call(
        attn_out_kernel,
        "attn_out",
        [
            ((half, width + 128), f32, False), ((half, width), f32, False), vec, vec, vec, vec,
            (qkv_bias.shape, f32, False), vec, (up_bias.shape, f32, False), vec,
        ],
        (ids, *outs[2], *near(tail)),
        room=6,
    )
    n0, n1, n2, n3, qb, ob, ub, db = small
    return (result[None], grad_inputs[None], n0, n1, n2, n3, g_qkv, qb, g_out, ob, g_up, ub, g_down, db)


def solution(mesh):
    token = P("fsdp", "ctx", None)
    vec = P("fsdp")
    mat = P("fsdp", None)
    return jax.shard_map(
        body,
        mesh=mesh,
        in_specs=(token, mat, vec, vec, vec, vec, mat, vec, mat, vec, mat, vec, mat, vec, token, token),
        out_specs=(token, token, vec, vec, vec, vec, mat, vec, mat, vec, mat, vec, mat, vec),
        check_vma=False,
    )
```

profile of v0, /device:TPU:0, one launch (start us, length us, event | category | flops | bytes accessed | tf_op | source)
XLA Modules:
  0.0 215.9 jit_solution(8061940902031129498)
XLA Ops:
  1.3 3.5 %pack.1 = (bf16[416,128]{1,0:T(8,128)(2,1)}, bf16[1568,128]{1,0:T(8,128)(2,1)}, bf16[704,768]{1,0:T(8,128)(2,1)}) custom-call(s32[4]{0:T(128)} %pad_add_fusion.ids.refs_0_, bf16[256,768]{1,0:T(8,128)(2,1)} %bitcast.9, bf16[256,768]{1,0:T(8,128)(2,1)} %bitcast.16, bf16[384,896]{1,0:T(8,128)(2,1)} %w.11, bf16[384,896]{1,0:T(8,128)(2,1)} %w.11, ...), custom_call_target="tpu_custom_call" | custom-call | flops 1 | bytes 1 | tf_op jit(solution)/shard_map/pack/pallas_call | solution.py:185
  8.4 8.8 %collective-permute-done.pu = bf16[1568,128]{1,0:T(8,128)(2,1)S(1)} collective-permute-done((bf16[1568,128]{1,0:T(8,128)(2,1)}, bf16[1568,128]{1,0:T(8,128)(2,1)S(1)}, u32[]{:S(2)}, u32[]{:S(2)}) %collective-permute-start) | collective-permute-done | bytes 401440 | tf_op jit(solution)/shard_map/ppermute | solution.py:78
  33.6 5.9 %collective-permute-done.4.refs_1_ = bf16[1024,128]{1,0:T(8,128)(2,1)S(1)} collective-permute-done((bf16[1024,128]{1,0:T(8,128)(2,1)S(1)}, bf16[1024,128]{1,0:T(8,128)(2,1)S(1)}, u32[]{:S(2)}, u32[]{:S(2)}) %collective-permute-start.4) | collective-permute-done | bytes 262176 | tf_op jit(solution)/shard_map/ppermute | solution.py:83
  39.5 3.0 %collective-permute-done.1.xd = bf16[704,768]{1,0:T(8,128)(2,1)S(1)} collective-permute-done((bf16[704,768]{1,0:T(8,128)(2,1)}, bf16[704,768]{1,0:T(8,128)(2,1)S(1)}, u32[]{:S(2)}, u32[]{:S(2)}) %collective-permute-start.1) | collective-permute-done | bytes 1081376 | tf_op jit(solution)/shard_map/ppermute | solution.py:78
  43.1 9.7 %ff.1 = (bf16[8,96,768]{2,1,0:T(8,128)(2,1)S(1)}, bf16[8,96,768]{2,1,0:T(8,128)(2,1)S(1)}, bf16[8,96,768]{2,1,0:T(8,128)(2,1)S(1)}, bf16[8,96,768]{2,1,0:T(8,128...) custom-call(s32[4]{0:T(128)S(1)} %copy-done.9, ...), custom_call_target="tpu_custom_call" | custom-call | flops 1 | bytes 1 | tf_op jit(solution)/shard_map/ff/pallas_call | solution.py:59
  63.7 8.6 %collective-permute-done.13.b_ref = bf16[4,96,768]{2,1,0:T(8,128)(2,1)S(1)} collective-permute-done((bf16[4,96,768]{2,1,0:T(8,128)(2,1)S(1)}, bf16[4,96,768]{2,1,0:T(8,128)(2,1)S(1)}, u32[]{:S(2)}, u32[]{:S(2)}) %collective-permute-start.13) | collective-permute-done | bytes 589856 | tf_op jit(solution)/shard_map/ppermute | solution.py:83
  76.1 8.0 %collective-permute-done.14.b_ref = bf16[4,96,768]{2,1,0:T(8,128)(2,1)S(1)} collective-permute-done((bf16[4,96,768]{2,1,0:T(8,128)(2,1)S(1)}, bf16[4,96,768]{2,1,0:T(8,128)(2,1)S(1)}, u32[]{:S(2)}, u32[]{:S(2)}) %collective-permute-start.14) | collective-permute-done | bytes 589856 | tf_op jit(solution)/shard_map/ppermute | solution.py:83
  85.8 3.7 %attn_forward.3 = (bf16[128,384]{1,0:T(8,128)(2,1)S(1)}, bf16[128,384]{1,0:T(8,128)(2,1)S(1)}, f32[3,16,128]{2,1,0:T(8,128)S(1)}) custom-call(s32[4]{0:T(128)S(1)} %copy-done.9, s32[1,16]{1,0:T(1,128)S(1)} %copy-done.11, bf16[256,768]{1,0:T(8,128)(2,1)S(1)} %get-tuple-element.152.q_ref.refs_2_, bf16[2048,128]{1,0:T(8,128)(2,1)S(1)} %kv_join.5.kv_mine.refs_3_, ...), custom_call_target="tpu_custom_call" | custom-call | flops 1000000000 | bytes 1 | tf_op jit(solution)/shard_map/attn_forward/pallas_call | solution.py:59
  89.6 3.3 %attn_backward.3 = (bf16[128,768]{1,0:T(8,128)(2,1)S(1)}, bf16[2048,128]{1,0:T(8,128)(2,1)S(1)}, bf16[2048,128]{1,0:T(8,128)(2,1)S(1)}) custom-call(s32[4]{0:T(128)S(1)} %copy-done.9, s32[1,16]{1,0:T(1,128)S(1)} %copy-done.11, bf16[256,768]{1,0:T(8,128)(2,1)S(1)} %get-tuple-element.152.q_ref.refs_2_, bf16[2048,128]{1,0:T(8,128)(2,1)S(1)} %kv_join.5.kv_mine.refs_3_, ...), custom_call_target="tpu_custom_call" | custom-call | flops 13000000512 | bytes 1 | tf_op jit(solution)/shard_map/attn_backward/pallas_call | solution.py:59
  94.7 17.9 %collective-permute-start.43 = (bf16[1,96,768]{2,1,0:T(8,128)(2,1)S(1)}, bf16[1,96,768]{2,1,0:T(8,128)(2,1)S(1)}, u32[]{:S(2)}, u32[]{:S(2)}) collective-permute-start(bf16[1,96,768]{2,1,0:T(8,128)(2,1)S(1)} %get-tuple-element.190), channel_id=1, source_target_pairs={{0,16},{2,18},{4,20},{6,22},{8,24},{10,26},{12,28},{14,30},{16,0},... | collective-permute-start | bytes 442376 | tf_op jit(solution)/shard_map/ppermute | solution.py:83
  112.9 8.7 %collective-permute-done.43.b = bf16[1,96,768]{2,1,0:T(8,128)(2,1)S(1)} collective-permute-done((bf16[1,96,768]{2,1,0:T(8,128)(2,1)S(1)}, bf16[1,96,768]{2,1,0:T(8,128)(2,1)S(1)}, u32[]{:S(2)}, u32[]{:S(2)}) %collective-permute-start.43) | collective-permute-done | bytes 147488 | tf_op jit(solution)/shard_map/ppermute | solution.py:83
  121.7 5.5 %ff_rest.1 = (f32[256,768]{1,0:T(8,128)S(1)}, f32[256,768]{1,0:T(8,128)S(1)}, f32[256,768]{1,0:T(8,128)S(1)}, bf16[256,768]{1,0:T(8,128)(2,1)S(1)}, f32[8,128]{1,0:T(8,128)S(1)}, /*index=5*/f32[8,128]{1,0:T(8,128)S(1)}) custom-call(s32[4]{0:T(128)S(1)} %copy-done.9, bf16[512,1536]{1,0:T(8,128)(2,1)S(1)} %get-tuple-element.119.act, ...), custom_call_target="tpu_custom_call" | custom-call | flops 1 | bytes 1 | tf_op jit(solution)/shard_map/ff_rest/pallas_call | solution.py:59
  129.9 3.0 %collective-permute-start.45 = (bf16[1,96,768]{2,1,0:T(8,128)(2,1)S(1)}, bf16[1,96,768]{2,1,0:T(8,128)(2,1)S(1)}, u32[]{:S(2)}, u32[]{:S(2)}) collective-permute-start(bf16[1,96,768]{2,1,0:T(8,128)(2,1)S(1)} %up_join.4.refs_0_), channel_id=1, source_target_pairs={{0,16},{2,18},{4,20},{6,22},{8,24},{10,26},{12,28},{14,30},{16,0},... | collective-permute-start | bytes 442376 | tf_op jit(solution)/shard_map/ppermute | solution.py:83
  134.6 4.5 %collective-permute-done.38.refs_1_ = bf16[1,96,768]{2,1,0:T(8,128)(2,1)S(1)} collective-permute-done((bf16[1,96,768]{2,1,0:T(8,128)(2,1)S(1)}, bf16[1,96,768]{2,1,0:T(8,128)(2,1)S(1)}, u32[]{:S(2)}, u32[]{:S(2)}) %collective-permute-start.38) | collective-permute-done | bytes 147488 | tf_op jit(solution)/shard_map/ppermute | solution.py:83
  140.7 4.8 %collective-permute-done.19.b_ref = bf16[1024,128]{1,0:T(8,128)(2,1)S(1)} collective-permute-done((bf16[1024,128]{1,0:T(8,128)(2,1)S(1)}, bf16[1024,128]{1,0:T(8,128)(2,1)S(1)}, u32[]{:S(2)}, u32[]{:S(2)}) %collective-permute-start.19) | collective-permute-done | bytes 262176 | tf_op jit(solution)/shard_map/ppermute | solution.py:83
  147.7 9.5 %collective-permute-done.20.b_ref = bf16[512,128]{1,0:T(8,128)(2,1)S(1)} collective-permute-done((bf16[512,128]{1,0:T(8,128)(2,1)S(1)}, bf16[512,128]{1,0:T(8,128)(2,1)S(1)}, u32[]{:S(2)}, u32[]{:S(2)}) %collective-permute-start.20) | collective-permute-done | bytes 131104 | tf_op jit(solution)/shard_map/ppermute | solution.py:83
  158.0 3.4 %collective-permute-start.22 = (bf16[256,128]{1,0:T(8,128)(2,1)S(1)}, bf16[256,128]{1,0:T(8,128)(2,1)S(1)}, u32[]{:S(2)}, u32[]{:S(2)}) collective-permute-start(bf16[256,128]{1,0:T(8,128)(2,1)S(1)} %get-tuple-element.168), channel_id=1, source_target_pairs={{0,16},{2,18},{4,20},{6,22},{8,24},{10,26},{12,28},{14,30},{16,0},... | collective-permute-start | bytes 196616 | tf_op jit(solution)/shard_map/ppermute | solution.py:83
  176.8 4.2 %collective-permute-done.27.refs_1_ = bf16[48,768]{1,0:T(8,128)(2,1)S(1)} collective-permute-done((bf16[48,768]{1,0:T(8,128)(2,1)S(1)}, bf16[48,768]{1,0:T(8,128)(2,1)S(1)}, u32[]{:S(2)}, u32[]{:S(2)}) %collective-permute-start.27) | collective-permute-done | bytes 73760 | tf_op jit(solution)/shard_map/ppermute | solution.py:83
  181.6 10.4 %collective-permute-done.47.refs_1_ = bf16[4,96,768]{2,1,0:T(8,128)(2,1)S(1)} collective-permute-done((bf16[4,96,768]{2,1,0:T(8,128)(2,1)S(1)}, bf16[4,96,768]{2,1,0:T(8,128)(2,1)S(1)}, u32[]{:S(2)}, u32[]{:S(2)}) %collective-permute-start.47) | collective-permute-done | bytes 589856 | tf_op jit(solution)/shard_map/ppermute | solution.py:83
  194.7 4.2 %collective-permute-done.29.refs_1_ = bf16[96,768]{1,0:T(8,128)(2,1)S(1)} collective-permute-done((bf16[96,768]{1,0:T(8,128)(2,1)S(1)}, bf16[96,768]{1,0:T(8,128)(2,1)S(1)}, u32[]{:S(2)}, u32[]{:S(2)}) %collective-permute-start.29) | collective-permute-done | bytes 147488 | tf_op jit(solution)/shard_map/ppermute | solution.py:83
  200.9 3.0 %collective-permute-start.49 = (bf16[416,128]{1,0:T(8,128)(2,1)S(1)}, bf16[416,128]{1,0:T(8,128)(2,1)S(1)}, u32[]{:S(2)}, u32[]{:S(2)}) collective-permute-start(bf16[416,128]{1,0:T(8,128)(2,1)S(1)} %tail_sum.6.refs_0_), channel_id=1, source_target_pairs={{0,16},{2,18},{4,20},{6,22},{8,24},{10,26},{12,28},{14,30},{16,0},... | collective-permute-start | bytes 319496 | tf_op jit(solution)/shard_map/ppermute | solution.py:83
  203.9 3.3 %collective-permute-done.30.refs_1_ = bf16[192,768]{1,0:T(8,128)(2,1)S(1)} collective-permute-done((bf16[192,768]{1,0:T(8,128)(2,1)S(1)}, bf16[192,768]{1,0:T(8,128)(2,1)S(1)}, u32[]{:S(2)}, u32[]{:S(2)}) %collective-permute-start.30) | collective-permute-done | bytes 294944 | tf_op jit(solution)/shard_map/ppermute | solution.py:83
  207.4 3.0 %down_out.1 = f32[1536,768]{1,0:T(8,128)} custom-call(s32[4]{0:T(128)S(1)} %copy-done.9, bf16[8,96,768]{2,1,0:T(8,128)(2,1)S(1)} %down_join.5.mine, bf16[8,96,768]{2,1,0:T(8,128)(2,1)S(1)} %collective-permute-done.41.theirs), custom_call_target="tpu_custom_call" | custom-call | flops 1 | bytes 1 | tf_op jit(solution)/shard_map/down_out/pallas_call | solution.py:59
  210.4 3.0 %up_out.1 = f32[384,3072]{1,0:T(8,128)} custom-call(s32[4]{0:T(128)S(1)} %copy-done.9, bf16[8,96,768]{2,1,0:T(8,128)(2,1)S(1)} %up_join.7.mine, bf16[8,96,768]{2,1,0:T(8,128)(2,1)S(1)} %collective-permute-done.48.theirs), custom_call_target="tpu_custom_call" | custom-call | flops 1 | bytes 1 | tf_op jit(solution)/shard_map/up_out/pallas_call | solution.py:59
  (168 shorter events, 71.5 us)
Async XLA Ops:
  4.8 12.4 %collective-permute-start = (bf16[1568,128]{1,0:T(8,128)(2,1)}, bf16[1568,128]{1,0:T(8,128)(2,1)S(1)}, u32[]{:S(2)}, u32[]{:S(2)}) collective-permute-start(bf16[1568,128]{1,0:T(8,128)(2,1)} %get-tuple-element.110), channel_id=1, source_target_pairs={{0,1},{1,0},{2,3},{3,2},{4,5},{5,4},{6,7},{7,6},{8,9},{9,8},{10,11... | collective-permute-start | bytes 1204232 | tf_op jit(solution)/shard_map/ppermute | solution.py:78
  17.2 25.3 %collective-permute-start.1 = (bf16[704,768]{1,0:T(8,128)(2,1)}, bf16[704,768]{1,0:T(8,128)(2,1)S(1)}, u32[]{:S(2)}, u32[]{:S(2)}) collective-permute-start(bf16[704,768]{1,0:T(8,128)(2,1)} %get-tuple-element.111), channel_id=1, source_target_pairs={{0,1},{1,0},{2,3},{3,2},{4,5},{5,4},{6,7},{7,6},{8,9},{9,8},{10,11... | collective-permute-start | bytes 3244040 | tf_op jit(solution)/shard_map/ppermute | solution.py:78
  29.6 13.5 %collective-permute-start.6 = (bf16[384,384]{1,0:T(8,128)(2,1)S(1)}, bf16[384,384]{1,0:T(8,128)(2,1)S(1)}, u32[]{:S(2)}, u32[]{:S(2)}) collective-permute-start(bf16[384,384]{1,0:T(8,128)(2,1)S(1)} %get-tuple-element.116.up0), channel_id=1, source_target_pairs={{0,2},{2,0},{4,6},{6,4},{8,10},{10,8},{12,14},{14,12},{16,18},{18,... | collective-permute-start | bytes 884744 | tf_op jit(solution)/shard_map/ppermute | solution.py:83
  29.6 13.5 %collective-permute-start.7 = (bf16[384,384]{1,0:T(8,128)(2,1)S(1)}, bf16[384,384]{1,0:T(8,128)(2,1)S(1)}, u32[]{:S(2)}, u32[]{:S(2)}) collective-permute-start(bf16[384,384]{1,0:T(8,128)(2,1)S(1)} %collective-permute-done.5.up1), channel_id=1, source_target_pairs={{0,2},{2,0},{4,6},{6,4},{8,10},{10,8},{12,14},{14,12},{16,18},{18,... | collective-permute-start | bytes 884744 | tf_op jit(solution)/shard_map/ppermute | solution.py:83
  56.0 16.2 %collective-permute-start.13 = (bf16[4,96,768]{2,1,0:T(8,128)(2,1)S(1)}, bf16[4,96,768]{2,1,0:T(8,128)(2,1)S(1)}, u32[]{:S(2)}, u32[]{:S(2)}) collective-permute-start(bf16[4,96,768]{2,1,0:T(8,128)(2,1)S(1)} %get-tuple-element.128), channel_id=1, source_target_pairs={{0,4},{2,6},{4,0},{6,2},{8,12},{10,14},{12,8},{14,10},{16,20},{18,... | collective-permute-start | bytes 1769480 | tf_op jit(solution)/shard_map/ppermute | solution.py:83
  59.6 24.5 %collective-permute-start.14 = (bf16[4,96,768]{2,1,0:T(8,128)(2,1)S(1)}, bf16[4,96,768]{2,1,0:T(8,128)(2,1)S(1)}, u32[]{:S(2)}, u32[]{:S(2)}) collective-permute-start(bf16[4,96,768]{2,1,0:T(8,128)(2,1)S(1)} %get-tuple-element.131), channel_id=1, source_target_pairs={{0,4},{2,6},{4,0},{6,2},{8,12},{10,14},{12,8},{14,10},{16,20},{18,... | collective-permute-start | bytes 1769480 | tf_op jit(solution)/shard_map/ppermute | solution.py:83
  72.4 17.2 %collective-permute-start.15 = (bf16[2,96,768]{2,1,0:T(8,128)(2,1)S(1)}, bf16[2,96,768]{2,1,0:T(8,128)(2,1)S(1)}, u32[]{:S(2)}, u32[]{:S(2)}) collective-permute-start(bf16[2,96,768]{2,1,0:T(8,128)(2,1)S(1)} %get-tuple-element.139), channel_id=1, source_target_pairs={{0,8},{2,10},{4,12},{6,14},{8,0},{10,2},{12,4},{14,6},{16,24},{18,... | collective-permute-start | bytes 884744 | tf_op jit(solution)/shard_map/ppermute | solution.py:83
  93.0 36.9 %collective-permute-start.23 = (bf16[256,768]{1,0:T(8,128)(2,1)S(1)}, bf16[256,768]{1,0:T(8,128)(2,1)S(1)}, u32[]{:S(2)}, u32[]{:S(2)}) collective-permute-start(bf16[256,768]{1,0:T(8,128)(2,1)S(1)} %get-tuple-element.158.dm.dm_own), channel_id=1, source_target_pairs={{0,1},{1,0},{2,3},{3,2},{4,5},{5,4},{6,7},{7,6},{8,9},{9,8},{10,11... | collective-permute-start | bytes 1179656 | tf_op jit(solution)/shard_map/ppermute | solution.py:78
  94.7 26.9 %collective-permute-start.43 = (bf16[1,96,768]{2,1,0:T(8,128)(2,1)S(1)}, bf16[1,96,768]{2,1,0:T(8,128)(2,1)S(1)}, u32[]{:S(2)}, u32[]{:S(2)}) collective-permute-start(bf16[1,96,768]{2,1,0:T(8,128)(2,1)S(1)} %get-tuple-element.190), channel_id=1, source_target_pairs={{0,16},{2,18},{4,20},{6,22},{8,24},{10,26},{12,28},{14,30},{16,0},... | collective-permute-start | bytes 442376 | tf_op jit(solution)/shard_map/ppermute | solution.py:83
  112.6 16.7 %collective-permute-start.16 = (bf16[256,384]{1,0:T(8,128)(2,1)S(1)}, bf16[256,384]{1,0:T(8,128)(2,1)S(1)}, u32[]{:S(2)}, u32[]{:S(2)}) collective-permute-start(bf16[256,384]{1,0:T(8,128)(2,1)S(1)} %get-tuple-element.157), channel_id=1, source_target_pairs={{0,1},{1,0},{2,3},{3,2},{4,5},{5,4},{6,7},{7,6},{8,9},{9,8},{10,11... | collective-permute-start | bytes 589832 | tf_op jit(solution)/shard_map/ppermute | solution.py:78
  112.7 21.7 %collective-permute-start.18 = (bf16[2048,128]{1,0:T(8,128)(2,1)S(1)}, bf16[2048,128]{1,0:T(8,128)(2,1)S(1)}, u32[]{:S(2)}, u32[]{:S(2)}) collective-permute-start(bf16[2048,128]{1,0:T(8,128)(2,1)S(1)} %get-tuple-element.160), channel_id=1, source_target_pairs={{0,2},{2,0},{4,6},{6,4},{8,10},{10,8},{12,14},{14,12},{16,18},{18,... | collective-permute-start | bytes 1572872 | tf_op jit(solution)/shard_map/ppermute | solution.py:83
  112.7 14.6 %collective-permute-start.37 = (bf16[1,96,768]{2,1,0:T(8,128)(2,1)S(1)}, bf16[1,96,768]{2,1,0:T(8,128)(2,1)S(1)}, u32[]{:S(2)}, u32[]{:S(2)}) collective-permute-start(bf16[1,96,768]{2,1,0:T(8,128)(2,1)S(1)} %get-tuple-element.151), channel_id=1, source_target_pairs={{0,16},{2,18},{4,20},{6,22},{8,24},{10,26},{12,28},{14,30},{16,0},... | collective-permute-start | bytes 442376 | tf_op jit(solution)/shard_map/ppermute | solution.py:83
  127.2 37.2 %collective-permute-start.21 = (bf16[256,768]{1,0:T(8,128)(2,1)S(1)}, bf16[256,768]{1,0:T(8,128)(2,1)S(1)}, u32[]{:S(2)}, u32[]{:S(2)}) collective-permute-start(bf16[256,768]{1,0:T(8,128)(2,1)S(1)} %get-tuple-element.166), channel_id=1, source_target_pairs={{0,1},{1,0},{2,3},{3,2},{4,5},{5,4},{6,7},{7,6},{8,9},{9,8},{10,11... | collective-permute-start | bytes 1179656 | tf_op jit(solution)/shard_map/ppermute | solution.py:78
  129.8 31.7 %collective-permute-start.17 = (bf16[256,768]{1,0:T(8,128)(2,1)S(1)}, bf16[256,768]{1,0:T(8,128)(2,1)S(1)}, u32[]{:S(2)}, u32[]{:S(2)}) collective-permute-start(bf16[256,768]{1,0:T(8,128)(2,1)S(1)} %mix.1), channel_id=1, source_target_pairs={{0,1},{1,0},{2,3},{3,2},{4,5},{5,4},{6,7},{7,6},{8,9},{9,8},{10,11... | collective-permute-start | bytes 1179656 | tf_op jit(solution)/shard_map/ppermute | solution.py:78
  140.6 17.4 %collective-permute-start.39 = (bf16[2,96,768]{2,1,0:T(8,128)(2,1)S(1)}, bf16[2,96,768]{2,1,0:T(8,128)(2,1)S(1)}, u32[]{:S(2)}, u32[]{:S(2)}) collective-permute-start(bf16[2,96,768]{2,1,0:T(8,128)(2,1)S(1)} %down_join.3.refs_0_), channel_id=1, source_target_pairs={{0,8},{2,10},{4,12},{6,14},{8,0},{10,2},{12,4},{14,6},{16,24},{18,... | collective-permute-start | bytes 884744 | tf_op jit(solution)/shard_map/ppermute | solution.py:83
  145.4 19.0 %collective-permute-start.46 = (bf16[2,96,768]{2,1,0:T(8,128)(2,1)S(1)}, bf16[2,96,768]{2,1,0:T(8,128)(2,1)S(1)}, u32[]{:S(2)}, u32[]{:S(2)}) collective-permute-start(bf16[2,96,768]{2,1,0:T(8,128)(2,1)S(1)} %up_join.5.refs_0_), channel_id=1, source_target_pairs={{0,8},{2,10},{4,12},{6,14},{8,0},{10,2},{12,4},{14,6},{16,24},{18,... | collective-permute-start | bytes 884744 | tf_op jit(solution)/shard_map/ppermute | solution.py:83
  145.5 11.7 %collective-permute-start.20 = (bf16[512,128]{1,0:T(8,128)(2,1)S(1)}, bf16[512,128]{1,0:T(8,128)(2,1)S(1)}, u32[]{:S(2)}, u32[]{:S(2)}) collective-permute-start(bf16[512,128]{1,0:T(8,128)(2,1)S(1)} %get-tuple-element.164), channel_id=1, source_target_pairs={{0,8},{2,10},{4,12},{6,14},{8,0},{10,2},{12,4},{14,6},{16,24},{18,... | collective-permute-start | bytes 393224 | tf_op jit(solution)/shard_map/ppermute | solution.py:83
  157.2 13.1 %collective-permute-start.25 = (bf16[192,768]{1,0:T(8,128)(2,1)S(1)}, bf16[192,768]{1,0:T(8,128)(2,1)S(1)}, u32[]{:S(2)}, u32[]{:S(2)}) collective-permute-start(bf16[192,768]{1,0:T(8,128)(2,1)S(1)} %get-tuple-element.176), channel_id=1, source_target_pairs={{0,4},{2,6},{4,0},{6,2},{8,12},{10,14},{12,8},{14,10},{16,20},{18,... | collective-permute-start | bytes 884744 | tf_op jit(solution)/shard_map/ppermute | solution.py:83
  164.4 17.1 %collective-permute-start.40 = (bf16[4,96,768]{2,1,0:T(8,128)(2,1)S(1)}, bf16[4,96,768]{2,1,0:T(8,128)(2,1)S(1)}, u32[]{:S(2)}, u32[]{:S(2)}) collective-permute-start(bf16[4,96,768]{2,1,0:T(8,128)(2,1)S(1)} %down_join.4.refs_0_), channel_id=1, source_target_pairs={{0,4},{2,6},{4,0},{6,2},{8,12},{10,14},{12,8},{14,10},{16,20},{18,... | collective-permute-start | bytes 1769480 | tf_op jit(solution)/shard_map/ppermute | solution.py:83
  164.4 27.6 %collective-permute-start.47 = (bf16[4,96,768]{2,1,0:T(8,128)(2,1)S(1)}, bf16[4,96,768]{2,1,0:T(8,128)(2,1)S(1)}, u32[]{:S(2)}, u32[]{:S(2)}) collective-permute-start(bf16[4,96,768]{2,1,0:T(8,128)(2,1)S(1)} %up_join.6.refs_0_), channel_id=1, source_target_pairs={{0,4},{2,6},{4,0},{6,2},{8,12},{10,14},{12,8},{14,10},{16,20},{18,... | collective-permute-start | bytes 1769480 | tf_op jit(solution)/shard_map/ppermute | solution.py:83
  176.1 17.6 %collective-permute-start.35 = (bf16[416,128]{1,0:T(8,128)(2,1)S(1)}, bf16[416,128]{1,0:T(8,128)(2,1)S(1)}, u32[]{:S(2)}, u32[]{:S(2)}) collective-permute-start(bf16[416,128]{1,0:T(8,128)(2,1)S(1)} %tail_sum.4.refs_0_), channel_id=1, source_target_pairs={{0,4},{2,6},{4,0},{6,2},{8,12},{10,14},{12,8},{14,10},{16,20},{18,... | collective-permute-start | bytes 319496 | tf_op jit(solution)/shard_map/ppermute | solution.py:83
  181.6 25.8 %collective-permute-start.41 = (bf16[8,96,768]{2,1,0:T(8,128)(2,1)S(1)}, bf16[8,96,768]{2,1,0:T(8,128)(2,1)S(1)}, u32[]{:S(2)}, u32[]{:S(2)}) collective-permute-start(bf16[8,96,768]{2,1,0:T(8,128)(2,1)S(1)} %down_join.5.mine), channel_id=1, source_target_pairs={{0,2},{2,0},{4,6},{6,4},{8,10},{10,8},{12,14},{14,12},{16,18},{18,... | collective-permute-start | bytes 3538952 | tf_op jit(solution)/shard_map/ppermute | solution.py:83
  192.1 18.3 %collective-permute-start.48 = (bf16[8,96,768]{2,1,0:T(8,128)(2,1)S(1)}, bf16[8,96,768]{2,1,0:T(8,128)(2,1)S(1)}, u32[]{:S(2)}, u32[]{:S(2)}) collective-permute-start(bf16[8,96,768]{2,1,0:T(8,128)(2,1)S(1)} %up_join.7.mine), channel_id=1, source_target_pairs={{0,2},{2,0},{4,6},{6,4},{8,10},{10,8},{12,14},{14,12},{16,18},{18,... | collective-permute-start | bytes 3538952 | tf_op jit(solution)/shard_map/ppermute | solution.py:83
  200.9 12.6 %collective-permute-start.49 = (bf16[416,128]{1,0:T(8,128)(2,1)S(1)}, bf16[416,128]{1,0:T(8,128)(2,1)S(1)}, u32[]{:S(2)}, u32[]{:S(2)}) collective-permute-start(bf16[416,128]{1,0:T(8,128)(2,1)S(1)} %tail_sum.6.refs_0_), channel_id=1, source_target_pairs={{0,16},{2,18},{4,20},{6,22},{8,24},{10,26},{12,28},{14,30},{16,0},... | collective-permute-start | bytes 319496 | tf_op jit(solution)/shard_map/ppermute | solution.py:83
  (41 other events, 325.7 us)
where the time goes:
time: 216 us
  waiting for transfers between devices  93 us (43%)
  starting transfers between devices  67.2 us (31%)
  Pallas kernels  52 us (24%)
    ppermute x40, waiting for transfers between devices, swap_ctx(): return lax.ppermute(value, 'ctx', [(i, i ^ mask) for i in range(devices)])  81.2 us
    ppermute x40, starting transfers between devices, swap_ctx(): return lax.ppermute(value, 'ctx', [(i, i ^ mask) for i in range(devices)])  55 us
    pallas_call x51, Pallas kernels, call(): pl.pallas_call(kernel, out_shape=tuple((pltpu.VMEM(s, d) if n else jax.Sh...  48.5 us
    ppermute x10, starting transfers between devices, swap_x(): return lax.ppermute(value, 'fsdp', [(0, 1), (1, 0)])  12.2 us
    ppermute x10, waiting for transfers between devices, swap_x(): return lax.ppermute(value, 'fsdp', [(0, 1), (1, 0)])  11.8 us
  transfers between devices with their start and end apart: 50, of which 20 were waited for; matrix products, arithmetic and copies ran while one was open for 0% of the time, Pallas kernels for 17%

commit v1 on v0

--- a/solution.py
+++ b/solution.py
@@ -16,7 +16,7 @@
 TN = (((0,), (0,)), ((), ()))
 bf16 = jnp.bfloat16
 f32 = jnp.float32
-WEIGHT = {'kv_add': 6.0, 'dm_kv': 0.0, 'tail': 3.0, 'tail_sum': 6.0, 'pair': 4.0, 'pair_add': 7.0, 'pair_sum': 7.0, 'pair_join': 7.0, 'both': 7.0, 'both_join': 7.0, 'down_join': 3.0, 'up_out': 0.0, 'up_join': 0.0, 'cotangent': 0.0, 'query': 6.0, 'ff': 0.0, 'attn_backward': 13.0, 'front': 13.0, 'attn_forward': 1.0, 'down_add': 0.0}
+WEIGHT = {'pile': 8.0, 'up_add': 1.0, 'down_join': 6.0, 'dm_kv': 2.0, 'pair_sum': 4.0, 'ff_rest': 2.0, 'mix': 0.0, 'tail': 0.0}
 TINY = pl.CostEstimate(flops=1, transcendentals=0, bytes_accessed=1)
 
 
@@ -30,6 +30,9 @@
 
 def smem():
     return pl.BlockSpec(memory_space=pltpu.SMEM)
+
+
+CHAIN = []
 
 
 class Near:
@@ -46,6 +49,11 @@
 
 
 def call(kernel, name, outs, args, scratch=(), room=2):
+    args = list(args)
+    if CHAIN:
+        at = next(i for i, v in enumerate(args) if not isinstance(v, Raw) and getattr(v, "dtype", f32) != jnp.int32)
+        v = args[at]
+        args[at] = Near(after(v.value, CHAIN[0])) if isinstance(v, Near) else after(v, CHAIN[0])
     specs = [vmem() for _ in args]
     values = list(args)
     for i, v in enumerate(args):
@@ -56,7 +64,9 @@
             values[i] = pltpu.with_memory_space_constraint(v.value, pltpu.VMEM)
         elif v.dtype == jnp.int32:
             specs[i] = smem()
-    return pl.pallas_call(
+    if lax.axis_size("ctx") > LOW and name[:4] != "attn":
+        room += sum(int(np.prod(s)) * jnp.dtype(d).itemsize for s, d, _ in outs) >> 20
+    results = pl.pallas_call(
         kernel,
         out_shape=tuple(pltpu.VMEM(s, d) if n else jax.ShapeDtypeStruct(s, d) for s, d, n in outs),
         in_specs=specs,
@@ -68,6 +78,8 @@
         ),
         compiler_params=pltpu.CompilerParams(vmem_limit_bytes=room << 20),
     )(*values)
+    CHAIN[:] = [results[0]]
+    return results
 
 
 def lanes(start, size):
@@ -149,7 +161,7 @@
     return lax.psum(value, "ctx", axis_index_groups=groups)
 
 
-def pack_kernel(ids, x, dy, kv_w, q_w, up_w, g1, b1, g2, b2, ob, db, qb, small, first, second):
+def pack_kernel(ids, kv_w, up_w, g1, b1, g2, b2, ob, db, qb, small, first):
     small[:384, :] = kv_w[...]
     small[384:, :] = jnp.zeros((32, 128), bf16)
     row = 384
@@ -167,40 +179,51 @@
     first[:416, :] = small[...]
     for k in range(3):
         first[416 + 384 * k : 800 + 384 * k, :] = up_w[:, k * 128 : (k + 1) * 128]
+
+
+def pack_tokens_kernel(ids, x, dy, q_w, xd):
     tokens = x.shape[0]
-    second[:tokens] = x[...]
-    second[tokens : 2 * tokens] = dy[...]
+    xd[:tokens] = x[...]
+    xd[tokens : 2 * tokens] = dy[...]
     rows = q_w.shape[0] // 2
-    second[2 * tokens :, : 2 * rows] = q_w[:rows]
-    second[2 * tokens :, 2 * rows :] = q_w[rows:]
-
-
-def pack(ids, x, dy, qkv_weight, up_weight, vectors):
-    half, width = qkv_weight.shape[0], 2 * qkv_weight.shape[0]
-    tokens = x.shape[0]
-    step = up_weight.shape[1] // 8
-    token = pl.BlockSpec(x.shape, lambda i, s: (0, 0))
-    whole = [pl.BlockSpec(v.shape, lambda i, s: (0,)) for v in vectors]
-    outs = ((half + 32, 128), (half + 32 + 3 * half, 128), (2 * tokens + half // 2, width))
+    xd[2 * tokens :, : 2 * rows] = q_w[:rows]
+    xd[2 * tokens :, 2 * rows :] = q_w[rows:]
+
+
+def pack_call(kernel, name, ids, args, specs, outs):
     return pl.pallas_call(
-        pack_kernel,
+        kernel,
         out_shape=tuple(jax.ShapeDtypeStruct(s, bf16) for s in outs),
         grid_spec=pltpu.PrefetchScalarGridSpec(
             num_scalar_prefetch=1,
             grid=(1,),
-            in_specs=[
-                token,
-                token,
-                pl.BlockSpec((half, 128), lambda i, s: (0, width // 128)),
-                pl.BlockSpec((half, half), lambda i, s: (0, s[2])),
-                pl.BlockSpec((half, step), lambda i, s: (0, (1 - s[1]) * 4 + s[2] * 2 + s[3])),
-            ]
-            + whole,
+            in_specs=specs,
             out_specs=[pl.BlockSpec(s, lambda i, s: (0, 0)) for s in outs],
         ),
-        name="pack",
-        cost_estimate=TINY,
-    )(ids, x, dy, qkv_weight, qkv_weight, up_weight, *vectors)
+        name=name,
+        cost_estimate=pl.CostEstimate(
+            flops=int(WEIGHT.get(name, 0) * 1e9) + 1, transcendentals=0, bytes_accessed=1
+        ),
+    )(ids, *args)
+
+
+def pack(ids, qkv_weight, up_weight, vectors):
+    half, width = qkv_weight.shape[0], 2 * qkv_weight.shape[0]
+    step = up_weight.shape[1] // 8
+    specs = [
+        pl.BlockSpec((half, 128), lambda i, s: (0, width // 128)),
+        pl.BlockSpec((half, step), lambda i, s: (0, (1 - s[1]) * 4 + s[2] * 2 + s[3])),
+    ] + [pl.BlockSpec(v.shape, lambda i, s: (0,)) for v in vectors]
+    outs = ((half + 32, 128), (half + 32 + 3 * half, 128))
+    return pack_call(pack_kernel, "pack", ids, (qkv_weight, up_weight, *vectors), specs, outs)
+
+
+def pack_tokens(ids, x, dy, qkv_weight):
+    half, width = qkv_weight.shape[0], 2 * qkv_weight.shape[0]
+    token = pl.BlockSpec(x.shape, lambda i, s: (0, 0))
+    specs = [token, token, pl.BlockSpec((half, half), lambda i, s: (0, s[2]))]
+    outs = ((2 * x.shape[0] + half // 2, width),)
+    return pack_call(pack_tokens_kernel, "pack_tokens", ids, (x, dy, qkv_weight), specs, outs)
 
 
 def row_vector(block, first, count=3):
@@ -778,6 +801,10 @@
     ub[...] = row_vector(small, 19, 12).reshape(ub.shape[0])
 
 
+class Values:
+    pass
+
+
 def body(
     layer_input, doc_lengths, ln1_gain, ln1_bias, ln2_gain, ln2_bias, qkv_weight, qkv_bias,
     out_weight, out_bias, up_weight, up_bias, down_weight, down_bias, out_grad, kv_grad_later,
@@ -794,8 +821,9 @@
     x_own, dy_own = layer_input[0], out_grad[0]
 
     vectors = (ln1_gain, ln1_bias, ln2_gain, ln2_bias, out_bias, down_bias, qkv_bias)
-    p_own, pu_own, xd_own = pack(ids, x_own, dy_own, qkv_weight, up_weight, vectors)
+    p_own, pu_own = pack(ids, qkv_weight, up_weight, vectors)
     pu_oth = swap_x(pu_own)
+    xd_own = pack_tokens(ids, x_own, dy_own, after(qkv_weight, pu_own))[0]
     xd = swap_x(after(xd_own, pu_oth))
 
     offsets = jnp.arange(half_rows, dtype=jnp.int32)
@@ -813,197 +841,278 @@
     t_angles = places.reshape(2, 1, half_rows) * freq[None, :, None]
     cos_t, sin_t = jnp.cos(t_angles), jnp.sin(t_angles)
 
-    first_own, kv, p_oth, up0 = call(
-        front_kernel,
-        "front",
-        [
-            ((tokens, width), bf16, False), ((tokens, 128), bf16, True), (p_own.shape, bf16, False),
-            ((half, half), bf16, True),
-        ],
-        (ids, x_own, p_own, *near(pu_oth), *tables),
-    )
-    up1, up2 = swap_ctx(up0, 2), swap_ctx(up0, 1)
-    kv = gather_step(kv, stages[0][0], "kv_join")
-    ups = (up0, up1, up2, swap_ctx(after(up1, kv), 1))
-    for stride, _ in stages[1:-2]:
-        kv = gather_step(kv, stride, "kv_join")
-    kv_mine = gather_step(kv, 2, "kv_join")
-    kv_theirs = swap_ctx(kv_mine, 1)
-
-    g_own, g_send, q_mine = call(
-        cotangent_kernel,
-        "cotangent",
-        [((tokens, half), bf16, False), ((tokens, half), bf16, True), ((half, half), bf16, True)],
-        (dy_own, *near(xd), out_weight),
-    )
-    g_oth = swap_x(g_send)
-    q_theirs = swap_ctx(q_mine, 1)
-
+    low = min(LOW, devices)
     rows = half // 4
     step = wide // 4
-    chunks = ((8, rows, width), bf16, True)
     token_f32, token_low = ((tokens, width), f32, False), ((tokens, width), bf16, False)
-    (
-        keep_a, send_a, keep_b, send_b, act, dh, hat_oth, first_oth, hat_half, dy_far, up_sum,
-    ) = call(
-        ff_kernel,
-        "ff",
-        [
-            chunks, chunks, chunks, chunks, ((2 * tokens, wide), bf16, True), ((2 * tokens, wide), bf16, True),
-            token_f32, token_low, ((tokens, half), f32, False), token_low, ((1, wide), f32, False),
-        ],
+    e = Values()
+    e.o, e.o_send, e.st, e.dm = {}, {}, {}, {}
+    e.down, e.up, e.kv, e.pair, e.tail = (Values() for _ in range(5))
+
+    def front():
+        e.first_own, kv, e.p_oth, up0 = call(
+            front_kernel,
+            "front",
+            [
+                ((tokens, width), bf16, False), ((tokens, 128), bf16, True), (p_own.shape, bf16, False),
+                ((half, half), bf16, True),
+            ],
+            (ids, x_own, p_own, *near(pu_oth), *tables),
+        )
+        up1 = swap_ctx(up0, 2)
+        e.ups = (up0, up1, swap_ctx(up0, 1), swap_ctx(up1, 1))
+        for stride, _ in stages[:-1]:
+            kv = gather_step(kv, stride, "kv_join")
+        e.kv_all = (kv, swap_ctx(kv, 1))
+
+    def cotangent():
+        e.g_own, g_send, e.q_mine = call(
+            cotangent_kernel,
+            "cotangent",
+            [((tokens, half), bf16, False), ((tokens, half), bf16, True), ((half, half), bf16, True)],
+            (dy_own, *near(xd), out_weight),
+        )
+        e.g_oth = swap_x(g_send)
+        e.q_theirs = swap_ctx(e.q_mine, 1)
+
+    def ff():
+        chunks = ((8, rows, width), bf16, True)
         (
-            ids, x_own, *near(after(xd, kv_mine, g_send)), dy_own, Raw(up_weight), *near(*ups), Raw(down_weight),
-            up_bias, p_own, p_oth,
-        ),
-        scratch=[
-            pltpu.VMEM((2 * tokens, width), bf16),
-            pltpu.VMEM((2 * tokens, width), bf16),
-            pltpu.VMEM((1, wide), f32),
-            pltpu.VMEM((half, width), bf16),
-            pltpu.VMEM((half, width), bf16),
-            pltpu.VMEM((4, half, step), bf16),
-            pltpu.VMEM((4, step, width), bf16),
-            pltpu.SemaphoreType.DMA((4,)),
-            pltpu.SemaphoreType.DMA((4,)),
-        ],
-        room=16,
-    )
-    row_block = ((8, 128), f32, False)
-    ff_own, ff_oth, ds_own, ds_oth, n_mine, n_send = call(
-        ff_rest_kernel,
-        "ff_rest",
-        [token_f32, token_f32, token_f32, token_low, row_block, row_block],
-        (ids, *near(act, dh), x_own, hat_oth, Raw(up_weight), *near(*ups), Raw(down_weight)),
-        scratch=[
-            pltpu.VMEM((8, width), f32),
-            pltpu.VMEM((4, half, step), bf16),
-            pltpu.VMEM((4, step, width), bf16),
-            pltpu.SemaphoreType.DMA((4,)),
-            pltpu.SemaphoreType.DMA((4,)),
-        ],
-        room=18,
-    )
-    n_recv = swap_x(n_send)
-    ds_recv = swap_x(ds_oth)
-    low = min(LOW, devices)
-    keep_a, send_a = scatter_step(keep_a, send_a, 1, "down_add")
-    keep_b, send_b = scatter_step(keep_b, send_b, 1, "up_add")
-    q, q_far = call(
-        query_kernel,
-        "query",
-        [((tokens, width), bf16, True), ((half, width), bf16, False)],
-        (ids, first_own, qkv_weight, *near(q_mine, q_theirs), p_own, p_oth, *tables),
-        scratch=[pltpu.VMEM((1, width), f32)],
-    )
+            keep_a, send_a, keep_b, send_b, e.act, e.dh, e.hat_oth, e.first_oth, e.hat_half,
+            e.dy_far, e.up_sum,
+        ) = call(
+            ff_kernel,
+            "ff",
+            [
+                chunks, chunks, chunks, chunks, ((2 * tokens, wide), bf16, True), ((2 * tokens, wide), bf16, True),
+                token_f32, token_low, ((tokens, half), f32, False), token_low, ((1, wide), f32, False),
+            ],
+            (
+                ids, x_own, *near(xd), dy_own, Raw(up_weight), *near(*e.ups), Raw(down_weight), up_bias, p_own,
+                e.p_oth,
+            ),
+            scratch=[
+                pltpu.VMEM((2 * tokens, width), bf16),
+                pltpu.VMEM((2 * tokens, width), bf16),
+                pltpu.VMEM((1, wide), f32),
+                pltpu.VMEM((half, width), bf16),
+                pltpu.VMEM((half, width), bf16),
+                pltpu.VMEM((4, half, step), bf16),
+                pltpu.VMEM((4, step, width), bf16),
+                pltpu.SemaphoreType.DMA((4,)),
+                pltpu.SemaphoreType.DMA((4,)),
+            ],
+            room=16,
+        )
+        e.down.parts, e.up.parts = (keep_a, swap_ctx(send_a, 1)), (keep_b, swap_ctx(send_b, 1))
+
+    def add_step(chain, mask, name):
+        kept, arrived = chain.parts
+        out = ((kept.shape[0] // 2,) + kept.shape[1:], kept.dtype, True)
+        kept, send = call(add_split_kernel, name, [out, out], near(kept, arrived))
+        chain.parts = (kept, swap_ctx(send, mask))
+
+    def join_step(chain, mask, name):
+        value, arrived = chain.parts
+        value = join(value, arrived, name)
+        chain.parts = (value, swap_ctx(value, mask))
+
+    def query():
+        e.q, e.q_far = call(
+            query_kernel,
+            "query",
+            [((tokens, width), bf16, True), ((half, width), bf16, False)],
+            (ids, e.first_own, qkv_weight, *near(e.q_mine, e.q_theirs), p_own, e.p_oth, *tables),
+            scratch=[pltpu.VMEM((1, width), f32)],
+        )
+
     pairs = (stages, devices, ids, doc_lengths)
-    q = after(q, send_a, send_b)
-    kv_all = (kv_mine, kv_theirs)
-    o_own0, o_send0, st0 = attn_forward(0, *pairs, q, kv_all, g_own, g_oth)
-    keep_a, send_a = scatter_step(after(keep_a, st0), send_a, 2, "down_add")
-    dm_own0, dkv = attn_backward(0, *pairs, after(q, send_a), kv_all, g_own, g_oth, st0, cos_t, sin_t)
-    keep_b, send_b = scatter_step(after(keep_b, dm_own0), send_b, 2, "up_add")
-    o_own1, o_send1, st1 = attn_forward(1, *pairs, after(q, send_b), kv_all, g_own, g_oth)
-    keep_a, send_a = scatter_step(after(keep_a, st1), send_a, 4, "down_add")
-    if devices <= LOW:
-        dm_own1, dkv_keep, dkv_send = attn_backward(
-            1, *pairs, after(q, send_a), kv_all, g_own, g_oth, st1, cos_t, sin_t, before=(dkv,)
+
+    def forward(side):
+        e.o[side], e.o_send[side], e.st[side] = attn_forward(
+            side, *pairs, e.q, e.kv_all, e.g_own, e.g_oth
         )
-    else:
-        dm_own1, dkv_more = attn_backward(1, *pairs, after(q, send_a), kv_all, g_own, g_oth, st1, cos_t, sin_t)
-        dkv = (dkv + dkv_more).astype(bf16)
-        dkv_keep, dkv_send = dkv[: kv_mine.shape[0]], dkv[kv_mine.shape[0] :]
-    keep_b, send_b = scatter_step(after(keep_b, dm_own1), send_b, 4, "up_add")
-    down_part = high_sum(sum_of(*scatter(keep_a, send_a, low, "down_add", 8), "down_sum"))
-    up_own, up_send = call(
-        up_part_kernel,
-        "up_part",
-        [((1, rows, half), bf16, True), ((1, rows, half), bf16, True)],
-        near(*scatter(keep_b, send_b, low, "up_add", 8)),
-    )
-    up_own, up_send = high_sum(up_own), high_sum(up_send)
-    up_part = call(up_join_kernel, "up_join", [((1, rows, width), bf16, True)], near(up_own, swap_x(up_send)))[0]
-    o_own, o_send, dm_own = call(
-        pile_kernel,
-        "pile",
-        [((tokens, half), bf16, False), ((tokens, half), bf16, True), ((tokens, width), bf16, True)],
-        (o_own0, o_own1, *near(o_send0, o_send1, dm_own0, dm_own1)),
-    )
-    kv_pieces = scatter(dkv_keep, dkv_send, devices, "kv_add")
-    o_oth = swap_x(o_send)
-    dm_oth = swap_x(dm_own)
-
-    y_send = call(mix_kernel, "mix", [((tokens, width), bf16, True)], (ff_oth, *near(o_oth), out_weight))[0]
-    y_recv = swap_x(y_send)
-    result = call(
-        result_kernel,
-        "result",
-        [((tokens, width), bf16, False)],
-        (ids, x_own, ff_own, o_own, out_weight, *near(y_recv), p_own, p_oth),
-    )[0]
-
-    kv_pieces = (after(kv_pieces[0], ds_recv), kv_pieces[1])
-    dm_kv = call(
-        dm_kv_kernel, "dm_kv", [((tokens, 128), bf16, True)], (*near(*kv_pieces), kv_grad_later[0], *tables)
-    )[0]
-    dm_kv_oth = swap_x(dm_kv)
-    grad_inputs = call(
-        x_grad_kernel,
-        "x_grad",
-        [((tokens, width), f32, False)],
-        (
-            ids, x_own, dy_own, *near(dm_own, dm_kv), qkv_weight, q_far, p_own, p_oth, ds_own,
-            *near(ds_recv),
-        ),
-        scratch=[pltpu.VMEM((tokens, width), f32)],
-        room=8,
-    )[0]
-    keep, send = call(
-        pair_kernel,
-        "pair",
-        [((half, width), bf16, True), ((half, width), bf16, True)],
-        (ids, first_own, first_oth, *near(dm_own, dm_oth), o_own, *near(o_oth), dy_own, dy_far),
-        scratch=[pltpu.VMEM((half, width), f32), pltpu.VMEM((half, width), f32)],
-        room=8,
-    )
-    pieces = scatter(keep, send, low, "pair_add")
-    pair = high_sum(sum_of(pieces[0], pieces[1], "pair_sum"))
-    tail = call(
-        tail_kernel,
-        "tail",
-        [((half + 32, 128), bf16, True)],
-        (
-            ids, first_own, first_oth, *near(dm_own, dm_oth), dy_own, dy_far, *near(dm_kv, dm_kv_oth), n_mine,
-            *near(n_recv), up_sum, x_own, hat_half, qkv_weight, p_own,
-        ),
-        scratch=[pltpu.VMEM((half + 32, 128), f32), pltpu.VMEM((tokens, width), f32)],
-        room=8,
-    )[0]
-    outs = []
-    for value, name in ((down_part, "down_join"), (up_part, "up_join"), (pair, "pair_join")):
-        for stride, _ in stages_of(low)[:-1]:
-            value = gather_step(value, stride, name)
-        outs.append(near(value, swap_ctx(value, 1)))
-    g_down = call(down_out_kernel, "down_out", [((wide, width), f32, False)], (ids, *outs[0]), room=8)[0]
-    g_up = call(up_out_kernel, "up_out", [((half, 2 * wide), f32, False)], (ids, *outs[1]), room=8)[0]
-    for i, (stride, _) in enumerate(stages[::-1]):
-        other = swap_ctx(tail, stride)
-        if i == 2:
-            tail = after(tail, result, grad_inputs)
-        if i == 3:
-            tail = after(tail, g_down, g_up)
-        tail = sum_of(tail, other, "tail_sum")
-    vec = ((half,), f32, False)
-    g_qkv, g_out, *small = call(
-        attn_out_kernel,
-        "attn_out",
-        [
-            ((half, width + 128), f32, False), ((half, width), f32, False), vec, vec, vec, vec,
-            (qkv_bias.shape, f32, False), vec, (up_bias.shape, f32, False), vec,
-        ],
-        (ids, *outs[2], *near(tail)),
-        room=6,
-    )
+
+    def backward(side):
+        before = (e.dkv,) if side == 1 and devices <= LOW else ()
+        e.dm[side], *dkv = attn_backward(
+            side, *pairs, e.q, e.kv_all, e.g_own, e.g_oth, e.st[side], cos_t, sin_t, before=before
+        )
+        if side == 0:
+            e.dkv = dkv[0]
+            return
+        if devices > LOW:
+            dkv = (e.dkv + dkv[0]).astype(bf16)
+            middle = dkv.shape[0] // 2
+            dkv = (dkv[:middle], dkv[middle:])
+        e.kv.parts = (dkv[0], swap_ctx(dkv[1], 1))
+
+    def pile():
+        e.o_own, o_send, e.dm_own = call(
+            pile_kernel,
+            "pile",
+            [((tokens, half), bf16, False), ((tokens, half), bf16, True), ((tokens, width), bf16, True)],
+            (e.o[0], e.o[1], *near(e.o_send[0], e.o_send[1], e.dm[0], e.dm[1])),
+        )
+        e.dm_oth, e.o_oth = swap_x(e.dm_own), swap_x(o_send)
+
+    def kv_more():
+        stride = 16
+        while stride < devices:
+            add_step(e.kv, stride, "kv_add")
+            stride *= 2
+
+    def ff_rest():
+        row_block = ((8, 128), f32, False)
+        e.ff_own, e.ff_oth, e.ds_own, ds_oth, e.n_mine, n_send = call(
+            ff_rest_kernel,
+            "ff_rest",
+            [token_f32, token_f32, token_f32, token_low, row_block, row_block],
+            (ids, *near(e.act, e.dh), x_own, e.hat_oth, Raw(up_weight), *near(*e.ups), Raw(down_weight)),
+            scratch=[
+                pltpu.VMEM((8, width), f32),
+                pltpu.VMEM((4, half, step), bf16),
+                pltpu.VMEM((4, step, width), bf16),
+                pltpu.SemaphoreType.DMA((4,)),
+                pltpu.SemaphoreType.DMA((4,)),
+            ],
+            room=18,
+        )
+        e.n_recv, e.ds_recv = swap_x(n_send), swap_x(ds_oth)
+
+    def down_sum():
+        value = high_sum(sum_of(*e.down.parts, "down_sum"))
+        e.down.parts = (value, swap_ctx(value, low // 2))
+
+    def up_part():
+        part = ((1, rows, half), bf16, True)
+        own, send = call(up_part_kernel, "up_part", [part, part], near(*e.up.parts))
+        own, send = high_sum(own), high_sum(send)
+        e.up.parts = (own, swap_x(send))
+
+    def up_join():
+        value = call(up_join_kernel, "up_join", [((1, rows, width), bf16, True)], near(*e.up.parts))[0]
+        e.up.parts = (value, swap_ctx(value, low // 2))
+
+    def pair():
+        keep, send = call(
+            pair_kernel,
+            "pair",
+            [((half, width), bf16, True), ((half, width), bf16, True)],
+            (
+                ids, e.first_own, e.first_oth, *near(e.dm_own, e.dm_oth), e.o_own, *near(e.o_oth),
+                dy_own, e.dy_far,
+            ),
+            scratch=[pltpu.VMEM((half, width), f32), pltpu.VMEM((half, width), f32)],
+            room=8,
+        )
+        e.pair.parts = (keep, swap_ctx(send, 1))
+
+    def pair_sum():
+        value = high_sum(sum_of(*e.pair.parts, "pair_sum"))
+        e.pair.parts = (value, swap_ctx(value, low // 2))
+
+    def mix():
+        y_send = call(
+            mix_kernel, "mix", [((tokens, width), bf16, True)], (e.ff_oth, *near(e.o_oth), out_weight)
+        )[0]
+        e.y_recv = swap_x(y_send)
+
+    def result():
+        e.result = call(
+            result_kernel,
+            "result",
+            [token_low],
+            (ids, x_own, e.ff_own, e.o_own, out_weight, *near(e.y_recv), p_own, e.p_oth),
+        )[0]
+
+    def dm_kv():
+        e.dm_kv = call(
+            dm_kv_kernel, "dm_kv", [((tokens, 128), bf16, True)], (*near(*e.kv.parts), kv_grad_later[0], *tables)
+        )[0]
+        e.dm_kv_oth = swap_x(e.dm_kv)
+
+    def x_grad():
+        e.x_grad = call(
+            x_grad_kernel,
+            "x_grad",
+            [token_f32],
+            (
+                ids, x_own, dy_own, *near(e.dm_own, e.dm_kv), qkv_weight, e.q_far, p_own, e.p_oth,
+                e.ds_own, *near(e.ds_recv),
+            ),
+            scratch=[pltpu.VMEM((tokens, width), f32)],
+            room=8,
+        )[0]
+
+    def tail():
+        value = call(
+            tail_kernel,
+            "tail",
+            [((half + 32, 128), bf16, True)],
+            (
+                ids, e.first_own, e.first_oth, *near(e.dm_own, e.dm_oth), dy_own, e.dy_far,
+                *near(e.dm_kv, e.dm_kv_oth), e.n_mine, *near(e.n_recv), e.up_sum, x_own,
+                e.hat_half, qkv_weight, p_own,
+            ),
+            scratch=[pltpu.VMEM((half + 32, 128), f32), pltpu.VMEM((tokens, width), f32)],
+            room=8,
+        )[0]
+        e.tail.parts = (value, swap_ctx(value, 1))
+
+    def tail_step(stride):
+        value = sum_of(*e.tail.parts, "tail_sum")
+        e.tail.parts = (value, swap_ctx(value, stride)) if stride < devices else (value,)
+
+    def tail_last():
+        stride = 16
+        while stride < devices:
+            tail_step(stride)
+            stride *= 2
+        tail_step(devices)
+
+    def down_out():
+        e.g_down = call(down_out_kernel, "down_out", [((wide, width), f32, False)], (ids, *near(*e.down.parts)), room=8)[0]
+
+    def up_out():
+        e.g_up = call(up_out_kernel, "up_out", [((half, 2 * wide), f32, False)], (ids, *near(*e.up.parts)), room=8)[0]
+
+    def attn_out():
+        vec = ((half,), f32, False)
+        e.small = call(
+            attn_out_kernel,
+            "attn_out",
+            [
+                ((half, width + 128), f32, False), ((half, width), f32, False), vec, vec, vec, vec,
+                (qkv_bias.shape, f32, False), vec, (up_bias.shape, f32, False), vec,
+            ],
+            (ids, *near(*e.pair.parts), *near(*e.tail.parts)),
+            room=6,
+        )
+
+    def steps(function, chain, masks, name):
+        return [partial(function, chain, mask, name) for mask in masks]
+
+    halves, shares = (2, 4, 8), (low // 4, low // 8, low // 16)
+    down_add, up_add = steps(add_step, e.down, halves, "down_add"), steps(add_step, e.up, halves, "up_add")
+    pair_add, kv_add = steps(add_step, e.pair, halves, "pair_add"), steps(add_step, e.kv, halves, "kv_add")
+    down_join, up_join_steps = steps(join_step, e.down, shares, "down_join"), steps(join_step, e.up, shares, "up_join")
+    pair_join = steps(join_step, e.pair, shares, "pair_join")
+    tail_add = [partial(tail_step, mask) for mask in halves]
+    order = [
+        front, cotangent, ff, down_add[0], up_add[0], query, partial(forward, 0), down_add[1],
+        partial(backward, 0), down_add[2], up_add[1], partial(forward, 1), partial(backward, 1), pile,
+        kv_add[0], down_sum, up_add[2], ff_rest, kv_add[1], pair, up_part, down_join[0], mix, pair_add[0],
+        kv_add[2], kv_more, up_join, dm_kv, pair_add[1], down_join[1], up_join_steps[0], pair_add[2], tail, x_grad,
+        tail_add[0], pair_sum, up_join_steps[1], tail_add[1], result, down_join[2], pair_join[0], pair_join[1],
+        tail_add[2], up_join_steps[2], tail_last, pair_join[2], attn_out, down_out, up_out,
+    ]
+    CHAIN.clear()
+    for run in order:
+        run()
+    CHAIN.clear()
+    result, grad_inputs, g_down, g_up = e.result, e.x_grad, e.g_down, e.g_up
+    g_qkv, g_out, *small = e.small
     n0, n1, n2, n3, qb, ob, ub, db = small
     return (result[None], grad_inputs[None], n0, n1, n2, n3, g_qkv, qb, g_out, ob, g_up, ub, g_down, db)
 

time: 216 us -> 202 us (0.935)
  Pallas kernels: 52 us -> 72.1 us
  starting transfers between devices: 67.2 us -> 50.2 us
  waiting for transfers between devices: 93 us -> 78.2 us
    ppermute x40, starting transfers between devices: 55 us -> 32.6 us  [swap_ctx(): return lax.ppermute(value, 'ctx', [(i, i ^ mask) for i in range(devices)])]
    ppermute x40, waiting for transfers between devices: 81.2 us -> 59.3 us  [swap_ctx(): return lax.ppermute(value, 'ctx', [(i, i ^ mask) for i in range(devices)])]
    pallas_call x51, Pallas kernels: 48.5 us -> 66.4 us  [call(): pl.pallas_call(kernel, out_shape=tuple((pltpu.VMEM(s, d) if n else jax.Sh...]
    ppermute x10, waiting for transfers between devices: 11.8 us -> 18.9 us  [swap_x(): return lax.ppermute(value, 'fsdp', [(0, 1), (1, 0)])]
    ppermute x10, starting transfers between devices: 12.2 us -> 17.6 us  [swap_x(): return lax.ppermute(value, 'fsdp', [(0, 1), (1, 0)])]
    pallas_call x1 -> x2, Pallas kernels: 3.48 us -> 5.62 us  [pack_call(): pl.pallas_call(kernel, out_shape=tuple((jax.ShapeDtypeStruct(s, bf16) for...]
  transfers between devices with their start and end apart: 50 -> 50, of which waited for: 20 -> 24; matrix products, arithmetic and copies ran while one was open for 0% -> 0% of each run, Pallas kernels for 17% -> 28%
where the time goes in v1:
time: 202 us; the launch traced here: 203 us
  waiting for transfers between devices  78.2 us (39%)
  Pallas kernels  72.1 us (36%)
  starting transfers between devices  50.2 us (25%)
    pallas_call x51, Pallas kernels, call(): pl.pallas_call(kernel, out_shape=tuple((pltpu.VMEM(s, d) if n else jax.Sh...  66.4 us
    ppermute x40, waiting for transfers between devices, swap_ctx(): return lax.ppermute(value, 'ctx', [(i, i ^ mask) for i in range(devices)])  59.3 us
    ppermute x40, starting transfers between devices, swap_ctx(): return lax.ppermute(value, 'ctx', [(i, i ^ mask) for i in range(devices)])  32.6 us
    ppermute x10, waiting for transfers between devices, swap_x(): return lax.ppermute(value, 'fsdp', [(0, 1), (1, 0)])  18.9 us
    ppermute x10, starting transfers between devices, swap_x(): return lax.ppermute(value, 'fsdp', [(0, 1), (1, 0)])  17.6 us
    pallas_call x2, Pallas kernels, pack_call(): pl.pallas_call(kernel, out_shape=tuple((jax.ShapeDtypeStruct(s, bf16) for...  5.62 us
  transfers between devices with their start and end apart: 50, of which 24 were waited for; matrix products, arithmetic and copies ran while one was open for 0% of the time, Pallas kernels for 28%

profile of v1, /device:TPU:0, one launch (start us, length us, event | category | flops | bytes accessed | tf_op | source)
XLA Modules:
  0.0 203.3 jit_solution(10846465968168575370)
XLA Ops:
  3.8 2.9 %collective-permute-start = (bf16[1568,128]{1,0:T(8,128)(2,1)}, bf16[1568,128]{1,0:T(8,128)(2,1)S(1)}, u32[]{:S(2)}, u32[]{:S(2)}) collective-permute-start(bf16[1568,128]{1,0:T(8,128)(2,1)} %get-tuple-element.146), channel_id=1, source_target_pairs={{0,1},{1,0},{2,3},{3,2},{4,5},{5,4},{6,7},{7,6},{8,9},{9,8},{10,11... | collective-permute-start | bytes 1204232 | tf_op jit(solution)/shard_map/ppermute | solution.py:90
  6.8 3.1 %pack_tokens.1 = bf16[704,768]{1,0:T(8,128)(2,1)} custom-call(s32[4]{0:T(128)} %pad_add_fusion.ids.refs_0_, bf16[256,768]{1,0:T(8,128)(2,1)} %bitcast.9, bf16[256,768]{1,0:T(8,128)(2,1)} %bitcast.16, bf16[384,896]{1,0:T(8,128)(2,1)} %w.10), custom_call_target="tpu_custom_call" | custom-call | flops 1 | bytes 1 | tf_op jit(solution)/shard_map/pack_tokens/pallas_call | solution.py:194
  9.9 6.4 %collective-permute-done.pu = bf16[1568,128]{1,0:T(8,128)(2,1)S(1)} collective-permute-done((bf16[1568,128]{1,0:T(8,128)(2,1)}, bf16[1568,128]{1,0:T(8,128)(2,1)S(1)}, u32[]{:S(2)}, u32[]{:S(2)}) %collective-permute-start) | collective-permute-done | bytes 401440 | tf_op jit(solution)/shard_map/ppermute | solution.py:90
  32.5 5.9 %collective-permute-done.3.refs_1_ = bf16[1024,128]{1,0:T(8,128)(2,1)S(1)} collective-permute-done((bf16[1024,128]{1,0:T(8,128)(2,1)S(1)}, bf16[1024,128]{1,0:T(8,128)(2,1)S(1)}, u32[]{:S(2)}, u32[]{:S(2)}) %collective-permute-start.3) | collective-permute-done | bytes 262176 | tf_op jit(solution)/shard_map/ppermute | solution.py:95
  38.4 3.1 %collective-permute-done.4.xd = bf16[704,768]{1,0:T(8,128)(2,1)S(1)} collective-permute-done((bf16[704,768]{1,0:T(8,128)(2,1)}, bf16[704,768]{1,0:T(8,128)(2,1)S(1)}, u32[]{:S(2)}, u32[]{:S(2)}) %collective-permute-start.4) | collective-permute-done | bytes 1081376 | tf_op jit(solution)/shard_map/ppermute | solution.py:90
  42.2 9.8 %ff.1 = (bf16[8,96,768]{2,1,0:T(8,128)(2,1)S(1)}, bf16[8,96,768]{2,1,0:T(8,128)(2,1)S(1)}, bf16[8,96,768]{2,1,0:T(8,128)(2,1)S(1)}, bf16[8,96,768]{2,1,0:T(8,128...) custom-call(s32[4]{0:T(128)S(1)} %copy-done.7, ...), custom_call_target="tpu_custom_call" | custom-call | flops 1 | bytes 1 | tf_op jit(solution)/shard_map/ff/pallas_call | solution.py:69
  61.4 3.7 %collective-permute-done.12.g_oth.refs_6_ = bf16[256,384]{1,0:T(8,128)(2,1)S(1)} collective-permute-done((bf16[256,384]{1,0:T(8,128)(2,1)S(1)}, bf16[256,384]{1,0:T(8,128)(2,1)S(1)}, u32[]{:S(2)}, u32[]{:S(2)}) %collective-permute-start.12) | collective-permute-done | bytes 196640 | tf_op jit(solution)/shard_map/ppermute | solution.py:90
  67.6 3.8 %collective-permute-done.13.b_ref = bf16[4,96,768]{2,1,0:T(8,128)(2,1)S(1)} collective-permute-done((bf16[4,96,768]{2,1,0:T(8,128)(2,1)S(1)}, bf16[4,96,768]{2,1,0:T(8,128)(2,1)S(1)}, u32[]{:S(2)}, u32[]{:S(2)}) %collective-permute-start.13) | collective-permute-done | bytes 589856 | tf_op jit(solution)/shard_map/ppermute | solution.py:95
  75.4 3.6 %collective-permute-done.14.b_ref = bf16[2,96,768]{2,1,0:T(8,128)(2,1)S(1)} collective-permute-done((bf16[2,96,768]{2,1,0:T(8,128)(2,1)S(1)}, bf16[2,96,768]{2,1,0:T(8,128)(2,1)S(1)}, u32[]{:S(2)}, u32[]{:S(2)}) %collective-permute-start.14) | collective-permute-done | bytes 294944 | tf_op jit(solution)/shard_map/ppermute | solution.py:95
  79.1 4.1 %collective-permute-done.15.b_ref = bf16[4,96,768]{2,1,0:T(8,128)(2,1)S(1)} collective-permute-done((bf16[4,96,768]{2,1,0:T(8,128)(2,1)S(1)}, bf16[4,96,768]{2,1,0:T(8,128)(2,1)S(1)}, u32[]{:S(2)}, u32[]{:S(2)}) %collective-permute-start.15) | collective-permute-done | bytes 589856 | tf_op jit(solution)/shard_map/ppermute | solution.py:95
  86.0 13.8 %attn_forward.3 = (bf16[128,384]{1,0:T(8,128)(2,1)S(1)}, bf16[128,384]{1,0:T(8,128)(2,1)S(1)}, f32[3,16,128]{2,1,0:T(8,128)S(1)}) custom-call(s32[4]{0:T(128)S(1)} %copy-done.7, s32[1,16]{1,0:T(1,128)S(1)} %copy-done.8, bf16[256,768]{1,0:T(8,128)(2,1)S(1)} %get-tuple-element.186.q_ref.refs_2_, bf16[2048,128]{1,0:T(8,128)(2,1)S(1)} %kv_join.5.kv_mine.refs_3_, ...), custom_call_target="tpu_custom_call" | custom-call | flops 1 | bytes 1 | tf_op jit(solution)/shard_map/attn_forward/pallas_call | solution.py:69
  99.7 11.1 %attn_backward.3 = (bf16[128,768]{1,0:T(8,128)(2,1)S(1)}, bf16[2048,128]{1,0:T(8,128)(2,1)S(1)}, bf16[2048,128]{1,0:T(8,128)(2,1)S(1)}) custom-call(s32[4]{0:T(128)S(1)} %copy-done.7, s32[1,16]{1,0:T(1,128)S(1)} %copy-done.8, bf16[256,768]{1,0:T(8,128)(2,1)S(1)} %get-tuple-element.186.q_ref.refs_2_, bf16[2048,128]{1,0:T(8,128)(2,1)S(1)} %kv_join.5.kv_mine.refs_3_, ...), custom_call_target="tpu_custom_call" | custom-call | flops 1 | bytes 1 | tf_op jit(solution)/shard_map/attn_backward/pallas_call | solution.py:69
  111.0 3.1 %collective-permute-start.20 = (bf16[256,768]{1,0:T(8,128)(2,1)S(1)}, bf16[256,768]{1,0:T(8,128)(2,1)S(1)}, u32[]{:S(2)}, u32[]{:S(2)}) collective-permute-start(bf16[256,768]{1,0:T(8,128)(2,1)S(1)} %get-tuple-element.213.dm_own.dm), channel_id=1, source_target_pairs={{0,1},{1,0},{2,3},{3,2},{4,5},{5,4},{6,7},{7,6},{8,9},{9,8},{10,11... | collective-permute-start | bytes 1179656 | tf_op jit(solution)/shard_map/ppermute | solution.py:90
  114.5 3.1 %collective-permute-done.18.b_ref = bf16[2,96,768]{2,1,0:T(8,128)(2,1)S(1)} collective-permute-done((bf16[2,96,768]{2,1,0:T(8,128)(2,1)S(1)}, bf16[2,96,768]{2,1,0:T(8,128)(2,1)S(1)}, u32[]{:S(2)}, u32[]{:S(2)}) %collective-permute-start.18) | collective-permute-done | bytes 294944 | tf_op jit(solution)/shard_map/ppermute | solution.py:95
  117.8 5.6 %ff_rest.1 = (f32[256,768]{1,0:T(8,128)S(1)}, f32[256,768]{1,0:T(8,128)S(1)}, f32[256,768]{1,0:T(8,128)S(1)}, bf16[256,768]{1,0:T(8,128)(2,1)S(1)}, f32[8,128]{1,0:T(8,128)S(1)}, /*index=5*/f32[8,128]{1,0:T(8,128)S(1)}) custom-call(s32[4]{0:T(128)S(1)} %copy-done.7, bf16[512,1536]{1,0:T(8,128)(2,1)S(1)} %get-tuple-element.204.act, ...), custom_call_target="tpu_custom_call" | custom-call | flops 2000000000 | bytes 1 | tf_op jit(solution)/shard_map/ff_rest/pallas_call | solution.py:69
  123.4 4.7 %collective-permute-done.21.o_oth.o = bf16[256,384]{1,0:T(8,128)(2,1)S(1)} collective-permute-done((bf16[256,384]{1,0:T(8,128)(2,1)S(1)}, bf16[256,384]{1,0:T(8,128)(2,1)S(1)}, u32[]{:S(2)}, u32[]{:S(2)}) %collective-permute-start.21) | collective-permute-done | bytes 196640 | tf_op jit(solution)/shard_map/ppermute | solution.py:90
  137.9 2.9 %collective-permute-start.30 = (bf16[1,96,768]{2,1,0:T(8,128)(2,1)S(1)}, bf16[1,96,768]{2,1,0:T(8,128)(2,1)S(1)}, u32[]{:S(2)}, u32[]{:S(2)}) collective-permute-start(bf16[1,96,768]{2,1,0:T(8,128)(2,1)S(1)} %up_join.4.refs_0_), channel_id=1, source_target_pairs={{0,16},{2,18},{4,20},{6,22},{8,24},{10,26},{12,28},{14,30},{16,0},... | collective-permute-start | bytes 442376 | tf_op jit(solution)/shard_map/ppermute | solution.py:95
  140.8 5.0 %collective-permute-done.27.refs_1_ = bf16[256,128]{1,0:T(8,128)(2,1)S(1)} collective-permute-done((bf16[256,128]{1,0:T(8,128)(2,1)S(1)}, bf16[256,128]{1,0:T(8,128)(2,1)S(1)}, u32[]{:S(2)}, u32[]{:S(2)}) %collective-permute-start.27) | collective-permute-done | bytes 65568 | tf_op jit(solution)/shard_map/ppermute | solution.py:95
  164.4 3.0 %collective-permute-done.37.refs_1_ = bf16[2,96,768]{2,1,0:T(8,128)(2,1)S(1)} collective-permute-done((bf16[2,96,768]{2,1,0:T(8,128)(2,1)S(1)}, bf16[2,96,768]{2,1,0:T(8,128)(2,1)S(1)}, u32[]{:S(2)}, u32[]{:S(2)}) %collective-permute-start.37) | collective-permute-done | bytes 294944 | tf_op jit(solution)/shard_map/ppermute | solution.py:95
  173.2 4.4 %collective-permute-done.42.refs_1_ = bf16[96,768]{1,0:T(8,128)(2,1)S(1)} collective-permute-done((bf16[96,768]{1,0:T(8,128)(2,1)S(1)}, bf16[96,768]{1,0:T(8,128)(2,1)S(1)}, u32[]{:S(2)}, u32[]{:S(2)}) %collective-permute-start.42) | collective-permute-done | bytes 147488 | tf_op jit(solution)/shard_map/ppermute | solution.py:95
  178.8 4.0 %collective-permute-done.44.refs_1_ = bf16[4,96,768]{2,1,0:T(8,128)(2,1)S(1)} collective-permute-done((bf16[4,96,768]{2,1,0:T(8,128)(2,1)S(1)}, bf16[4,96,768]{2,1,0:T(8,128)(2,1)S(1)}, u32[]{:S(2)}, u32[]{:S(2)}) %collective-permute-start.44) | collective-permute-done | bytes 589856 | tf_op jit(solution)/shard_map/ppermute | solution.py:95
  185.4 7.4 %collective-permute-done.45.refs_1_ = bf16[416,128]{1,0:T(8,128)(2,1)S(1)} collective-permute-done((bf16[416,128]{1,0:T(8,128)(2,1)S(1)}, bf16[416,128]{1,0:T(8,128)(2,1)S(1)}, u32[]{:S(2)}, u32[]{:S(2)}) %collective-permute-start.45) | collective-permute-done | bytes 106528 | tf_op jit(solution)/shard_map/ppermute | solution.py:95
  197.2 3.0 %down_out.1 = f32[1536,768]{1,0:T(8,128)} custom-call(s32[4]{0:T(128)S(1)} %copy-done.7, bf16[8,96,768]{2,1,0:T(8,128)(2,1)S(1)} %down_join.5.mine, bf16[8,96,768]{2,1,0:T(8,128)(2,1)S(1)} %collective-permute-done.48.theirs), custom_call_target="tpu_custom_call" | custom-call | flops 1 | bytes 1 | tf_op jit(solution)/shard_map/down_out/pallas_call | solution.py:69
  200.2 3.0 %up_out.1 = f32[384,3072]{1,0:T(8,128)} custom-call(s32[4]{0:T(128)S(1)} %copy-done.7, bf16[8,96,768]{2,1,0:T(8,128)(2,1)S(1)} %up_join.7.mine, bf16[8,96,768]{2,1,0:T(8,128)(2,1)S(1)} %collective-permute-done.49.theirs), custom_call_target="tpu_custom_call" | custom-call | flops 1 | bytes 1 | tf_op jit(solution)/shard_map/up_out/pallas_call | solution.py:69
  (167 shorter events, 81.5 us)
Async XLA Ops:
  3.8 12.4 %collective-permute-start = (bf16[1568,128]{1,0:T(8,128)(2,1)}, bf16[1568,128]{1,0:T(8,128)(2,1)S(1)}, u32[]{:S(2)}, u32[]{:S(2)}) collective-permute-start(bf16[1568,128]{1,0:T(8,128)(2,1)} %get-tuple-element.146), channel_id=1, source_target_pairs={{0,1},{1,0},{2,3},{3,2},{4,5},{5,4},{6,7},{7,6},{8,9},{9,8},{10,11... | collective-permute-start | bytes 1204232 | tf_op jit(solution)/shard_map/ppermute | solution.py:90
  16.3 25.3 %collective-permute-start.4 = (bf16[704,768]{1,0:T(8,128)(2,1)}, bf16[704,768]{1,0:T(8,128)(2,1)S(1)}, u32[]{:S(2)}, u32[]{:S(2)}) collective-permute-start(bf16[704,768]{1,0:T(8,128)(2,1)} %pack_tokens.1), channel_id=1, source_target_pairs={{0,1},{1,0},{2,3},{3,2},{4,5},{5,4},{6,7},{7,6},{8,9},{9,8},{10,11... | collective-permute-start | bytes 3244040 | tf_op jit(solution)/shard_map/ppermute | solution.py:90
  28.5 13.6 %collective-permute-start.6 = (bf16[384,384]{1,0:T(8,128)(2,1)S(1)}, bf16[384,384]{1,0:T(8,128)(2,1)S(1)}, u32[]{:S(2)}, u32[]{:S(2)}) collective-permute-start(bf16[384,384]{1,0:T(8,128)(2,1)S(1)} %get-tuple-element.157.up0), channel_id=1, source_target_pairs={{0,2},{2,0},{4,6},{6,4},{8,10},{10,8},{12,14},{14,12},{16,18},{18,... | collective-permute-start | bytes 884744 | tf_op jit(solution)/shard_map/ppermute | solution.py:95
  28.5 13.6 %collective-permute-start.7 = (bf16[384,384]{1,0:T(8,128)(2,1)S(1)}, bf16[384,384]{1,0:T(8,128)(2,1)S(1)}, u32[]{:S(2)}, u32[]{:S(2)}) collective-permute-start(bf16[384,384]{1,0:T(8,128)(2,1)S(1)} %collective-permute-done.5.up1), channel_id=1, source_target_pairs={{0,2},{2,0},{4,6},{6,4},{8,10},{10,8},{12,14},{14,12},{16,18},{18,... | collective-permute-start | bytes 884744 | tf_op jit(solution)/shard_map/ppermute | solution.py:95
  55.1 16.2 %collective-permute-start.13 = (bf16[4,96,768]{2,1,0:T(8,128)(2,1)S(1)}, bf16[4,96,768]{2,1,0:T(8,128)(2,1)S(1)}, u32[]{:S(2)}, u32[]{:S(2)}) collective-permute-start(bf16[4,96,768]{2,1,0:T(8,128)(2,1)S(1)} %get-tuple-element.173), channel_id=1, source_target_pairs={{0,4},{2,6},{4,0},{6,2},{8,12},{10,14},{12,8},{14,10},{16,20},{18,... | collective-permute-start | bytes 1769480 | tf_op jit(solution)/shard_map/ppermute | solution.py:95
  57.5 25.7 %collective-permute-start.15 = (bf16[4,96,768]{2,1,0:T(8,128)(2,1)S(1)}, bf16[4,96,768]{2,1,0:T(8,128)(2,1)S(1)}, u32[]{:S(2)}, u32[]{:S(2)}) collective-permute-start(bf16[4,96,768]{2,1,0:T(8,128)(2,1)S(1)} %get-tuple-element.182), channel_id=1, source_target_pairs={{0,4},{2,6},{4,0},{6,2},{8,12},{10,14},{12,8},{14,10},{16,20},{18,... | collective-permute-start | bytes 1769480 | tf_op jit(solution)/shard_map/ppermute | solution.py:95
  83.4 30.9 %collective-permute-start.17 = (bf16[1,96,768]{2,1,0:T(8,128)(2,1)S(1)}, bf16[1,96,768]{2,1,0:T(8,128)(2,1)S(1)}, u32[]{:S(2)}, u32[]{:S(2)}) collective-permute-start(bf16[1,96,768]{2,1,0:T(8,128)(2,1)S(1)} %get-tuple-element.200), channel_id=1, source_target_pairs={{0,16},{2,18},{4,20},{6,22},{8,24},{10,26},{12,28},{14,30},{16,0},... | collective-permute-start | bytes 442376 | tf_op jit(solution)/shard_map/ppermute | solution.py:95
  111.0 17.1 %collective-permute-start.20 = (bf16[256,768]{1,0:T(8,128)(2,1)S(1)}, bf16[256,768]{1,0:T(8,128)(2,1)S(1)}, u32[]{:S(2)}, u32[]{:S(2)}) collective-permute-start(bf16[256,768]{1,0:T(8,128)(2,1)S(1)} %get-tuple-element.213.dm_own.dm), channel_id=1, source_target_pairs={{0,1},{1,0},{2,3},{3,2},{4,5},{5,4},{6,7},{7,6},{8,9},{9,8},{10,11... | collective-permute-start | bytes 1179656 | tf_op jit(solution)/shard_map/ppermute | solution.py:90
  114.1 14.0 %collective-permute-start.21 = (bf16[256,384]{1,0:T(8,128)(2,1)S(1)}, bf16[256,384]{1,0:T(8,128)(2,1)S(1)}, u32[]{:S(2)}, u32[]{:S(2)}) collective-permute-start(bf16[256,384]{1,0:T(8,128)(2,1)S(1)} %get-tuple-element.214), channel_id=1, source_target_pairs={{0,1},{1,0},{2,3},{3,2},{4,5},{5,4},{6,7},{7,6},{8,9},{9,8},{10,11... | collective-permute-start | bytes 589832 | tf_op jit(solution)/shard_map/ppermute | solution.py:90
  114.4 16.5 %collective-permute-start.23 = (bf16[1,96,768]{2,1,0:T(8,128)(2,1)S(1)}, bf16[1,96,768]{2,1,0:T(8,128)(2,1)S(1)}, u32[]{:S(2)}, u32[]{:S(2)}) collective-permute-start(bf16[1,96,768]{2,1,0:T(8,128)(2,1)S(1)} %down_sum.1.refs_0_), channel_id=1, source_target_pairs={{0,16},{2,18},{4,20},{6,22},{8,24},{10,26},{12,28},{14,30},{16,0},... | collective-permute-start | bytes 442376 | tf_op jit(solution)/shard_map/ppermute | solution.py:95
  117.7 13.1 %collective-permute-start.22 = (bf16[1,96,768]{2,1,0:T(8,128)(2,1)S(1)}, bf16[1,96,768]{2,1,0:T(8,128)(2,1)S(1)}, u32[]{:S(2)}, u32[]{:S(2)}) collective-permute-start(bf16[1,96,768]{2,1,0:T(8,128)(2,1)S(1)} %get-tuple-element.219), channel_id=1, source_target_pairs={{0,16},{2,18},{4,20},{6,22},{8,24},{10,26},{12,28},{14,30},{16,0},... | collective-permute-start | bytes 442376 | tf_op jit(solution)/shard_map/ppermute | solution.py:95
  131.7 14.3 %collective-permute-start.28 = (bf16[192,768]{1,0:T(8,128)(2,1)S(1)}, bf16[192,768]{1,0:T(8,128)(2,1)S(1)}, u32[]{:S(2)}, u32[]{:S(2)}) collective-permute-start(bf16[192,768]{1,0:T(8,128)(2,1)S(1)} %get-tuple-element.234), channel_id=1, source_target_pairs={{0,4},{2,6},{4,0},{6,2},{8,12},{10,14},{12,8},{14,10},{16,20},{18,... | collective-permute-start | bytes 884744 | tf_op jit(solution)/shard_map/ppermute | solution.py:95
  131.8 14.4 %collective-permute-start.29 = (bf16[2,96,768]{2,1,0:T(8,128)(2,1)S(1)}, bf16[2,96,768]{2,1,0:T(8,128)(2,1)S(1)}, u32[]{:S(2)}, u32[]{:S(2)}) collective-permute-start(bf16[2,96,768]{2,1,0:T(8,128)(2,1)S(1)} %down_join.3.refs_0_), channel_id=1, source_target_pairs={{0,8},{2,10},{4,12},{6,14},{8,0},{10,2},{12,4},{14,6},{16,24},{18,... | collective-permute-start | bytes 884744 | tf_op jit(solution)/shard_map/ppermute | solution.py:95
  136.0 9.9 %collective-permute-start.27 = (bf16[256,128]{1,0:T(8,128)(2,1)S(1)}, bf16[256,128]{1,0:T(8,128)(2,1)S(1)}, u32[]{:S(2)}, u32[]{:S(2)}) collective-permute-start(bf16[256,128]{1,0:T(8,128)(2,1)S(1)} %get-tuple-element.232), channel_id=1, source_target_pairs={{0,16},{2,18},{4,20},{6,22},{8,24},{10,26},{12,28},{14,30},{16,0},... | collective-permute-start | bytes 196616 | tf_op jit(solution)/shard_map/ppermute | solution.py:95
  136.1 19.4 %collective-permute-start.34 = (bf16[256,768]{1,0:T(8,128)(2,1)S(1)}, bf16[256,768]{1,0:T(8,128)(2,1)S(1)}, u32[]{:S(2)}, u32[]{:S(2)}) collective-permute-start(bf16[256,768]{1,0:T(8,128)(2,1)S(1)} %get-tuple-element.249), channel_id=1, source_target_pairs={{0,1},{1,0},{2,3},{3,2},{4,5},{5,4},{6,7},{7,6},{8,9},{9,8},{10,11... | collective-permute-start | bytes 1179656 | tf_op jit(solution)/shard_map/ppermute | solution.py:90
  137.9 10.8 %collective-permute-start.30 = (bf16[1,96,768]{2,1,0:T(8,128)(2,1)S(1)}, bf16[1,96,768]{2,1,0:T(8,128)(2,1)S(1)}, u32[]{:S(2)}, u32[]{:S(2)}) collective-permute-start(bf16[1,96,768]{2,1,0:T(8,128)(2,1)S(1)} %up_join.4.refs_0_), channel_id=1, source_target_pairs={{0,16},{2,18},{4,20},{6,22},{8,24},{10,26},{12,28},{14,30},{16,0},... | collective-permute-start | bytes 442376 | tf_op jit(solution)/shard_map/ppermute | solution.py:95
  146.3 24.8 %collective-permute-start.40 = (bf16[4,96,768]{2,1,0:T(8,128)(2,1)S(1)}, bf16[4,96,768]{2,1,0:T(8,128)(2,1)S(1)}, u32[]{:S(2)}, u32[]{:S(2)}) collective-permute-start(bf16[4,96,768]{2,1,0:T(8,128)(2,1)S(1)} %down_join.4.refs_0_), channel_id=1, source_target_pairs={{0,4},{2,6},{4,0},{6,2},{8,12},{10,14},{12,8},{14,10},{16,20},{18,... | collective-permute-start | bytes 1769480 | tf_op jit(solution)/shard_map/ppermute | solution.py:95
  154.2 15.1 %collective-permute-start.39 = (bf16[256,768]{1,0:T(8,128)(2,1)S(1)}, bf16[256,768]{1,0:T(8,128)(2,1)S(1)}, u32[]{:S(2)}, u32[]{:S(2)}) collective-permute-start(bf16[256,768]{1,0:T(8,128)(2,1)S(1)} %mix.1), channel_id=1, source_target_pairs={{0,1},{1,0},{2,3},{3,2},{4,5},{5,4},{6,7},{7,6},{8,9},{9,8},{10,11... | collective-permute-start | bytes 1179656 | tf_op jit(solution)/shard_map/ppermute | solution.py:90
  155.5 11.9 %collective-permute-start.37 = (bf16[2,96,768]{2,1,0:T(8,128)(2,1)S(1)}, bf16[2,96,768]{2,1,0:T(8,128)(2,1)S(1)}, u32[]{:S(2)}, u32[]{:S(2)}) collective-permute-start(bf16[2,96,768]{2,1,0:T(8,128)(2,1)S(1)} %up_join.5.refs_0_), channel_id=1, source_target_pairs={{0,8},{2,10},{4,12},{6,14},{8,0},{10,2},{12,4},{14,6},{16,24},{18,... | collective-permute-start | bytes 884744 | tf_op jit(solution)/shard_map/ppermute | solution.py:95
  161.5 9.6 %collective-permute-start.41 = (bf16[48,768]{1,0:T(8,128)(2,1)S(1)}, bf16[48,768]{1,0:T(8,128)(2,1)S(1)}, u32[]{:S(2)}, u32[]{:S(2)}) collective-permute-start(bf16[48,768]{1,0:T(8,128)(2,1)S(1)} %pair_sum.1.refs_0_), channel_id=1, source_target_pairs={{0,16},{2,18},{4,20},{6,22},{8,24},{10,26},{12,28},{14,30},{16,0},... | collective-permute-start | bytes 221192 | tf_op jit(solution)/shard_map/ppermute | solution.py:95
  167.5 15.3 %collective-permute-start.44 = (bf16[4,96,768]{2,1,0:T(8,128)(2,1)S(1)}, bf16[4,96,768]{2,1,0:T(8,128)(2,1)S(1)}, u32[]{:S(2)}, u32[]{:S(2)}) collective-permute-start(bf16[4,96,768]{2,1,0:T(8,128)(2,1)S(1)} %up_join.6.refs_0_), channel_id=1, source_target_pairs={{0,4},{2,6},{4,0},{6,2},{8,12},{10,14},{12,8},{14,10},{16,20},{18,... | collective-permute-start | bytes 1769480 | tf_op jit(solution)/shard_map/ppermute | solution.py:95
  173.2 23.9 %collective-permute-start.48 = (bf16[8,96,768]{2,1,0:T(8,128)(2,1)S(1)}, bf16[8,96,768]{2,1,0:T(8,128)(2,1)S(1)}, u32[]{:S(2)}, u32[]{:S(2)}) collective-permute-start(bf16[8,96,768]{2,1,0:T(8,128)(2,1)S(1)} %down_join.5.mine), channel_id=1, source_target_pairs={{0,2},{2,0},{4,6},{6,4},{8,10},{10,8},{12,14},{14,12},{16,18},{18,... | collective-permute-start | bytes 3538952 | tf_op jit(solution)/shard_map/ppermute | solution.py:95
  182.9 17.3 %collective-permute-start.49 = (bf16[8,96,768]{2,1,0:T(8,128)(2,1)S(1)}, bf16[8,96,768]{2,1,0:T(8,128)(2,1)S(1)}, u32[]{:S(2)}, u32[]{:S(2)}) collective-permute-start(bf16[8,96,768]{2,1,0:T(8,128)(2,1)S(1)} %up_join.7.mine), channel_id=1, source_target_pairs={{0,2},{2,0},{4,6},{6,4},{8,10},{10,8},{12,14},{14,12},{16,18},{18,... | collective-permute-start | bytes 3538952 | tf_op jit(solution)/shard_map/ppermute | solution.py:95
  183.0 9.8 %collective-permute-start.46 = (bf16[192,768]{1,0:T(8,128)(2,1)S(1)}, bf16[192,768]{1,0:T(8,128)(2,1)S(1)}, u32[]{:S(2)}, u32[]{:S(2)}) collective-permute-start(bf16[192,768]{1,0:T(8,128)(2,1)S(1)} %pair_join.4.refs_0_), channel_id=1, source_target_pairs={{0,4},{2,6},{4,0},{6,2},{8,12},{10,14},{12,8},{14,10},{16,20},{18,... | collective-permute-start | bytes 884744 | tf_op jit(solution)/shard_map/ppermute | solution.py:95
  (40 other events, 332.2 us)

commit v2 on v1

--- a/solution.py
+++ b/solution.py
@@ -824,7 +824,7 @@
     p_own, pu_own = pack(ids, qkv_weight, up_weight, vectors)
     pu_oth = swap_x(pu_own)
     xd_own = pack_tokens(ids, x_own, dy_own, after(qkv_weight, pu_own))[0]
-    xd = swap_x(after(xd_own, pu_oth))
+    xd = swap_x(xd_own)
 
     offsets = jnp.arange(half_rows, dtype=jnp.int32)
     places = jnp.concatenate([me * half_rows + offsets, (2 * devices - 1 - me) * half_rows + offsets]).astype(f32)

time: 202 us -> 201 us (level); the launches traced: 203 us -> 200 us
  starting transfers between devices: 50.2 us -> 72.8 us
  Pallas kernels: 72.1 us -> 51.6 us
  waiting for transfers between devices: 78.2 us -> 73 us
    ppermute x40, starting transfers between devices: 32.6 us -> 61 us  [swap_ctx(): return lax.ppermute(value, 'ctx', [(i, i ^ mask) for i in range(devices)])]
    pallas_call x51, Pallas kernels: 66.4 us -> 46 us  [call(): pl.pallas_call(kernel, out_shape=tuple((pltpu.VMEM(s, d) if n else jax.Sh...]
    ppermute x10, starting transfers between devices: 17.6 us -> 11.7 us  [swap_x(): return lax.ppermute(value, 'fsdp', [(0, 1), (1, 0)])]
    ppermute x40, waiting for transfers between devices: 59.3 us -> 53.6 us  [swap_ctx(): return lax.ppermute(value, 'ctx', [(i, i ^ mask) for i in range(devices)])]
  transfers between devices with their start and end apart: 50 -> 50, of which waited for: 24 -> 25; matrix products, arithmetic and copies ran while one was open for 0% -> 0% of each run, Pallas kernels for 28% -> 18%
where the time goes in v2:
time: 201 us; the launch traced here: 200 us
  waiting for transfers between devices  73 us (36%)
  starting transfers between devices  72.8 us (36%)
  Pallas kernels  51.6 us (26%)
    ppermute x40, starting transfers between devices, swap_ctx(): return lax.ppermute(value, 'ctx', [(i, i ^ mask) for i in range(devices)])  61 us
    ppermute x40, waiting for transfers between devices, swap_ctx(): return lax.ppermute(value, 'ctx', [(i, i ^ mask) for i in range(devices)])  53.6 us
    pallas_call x51, Pallas kernels, call(): pl.pallas_call(kernel, out_shape=tuple((pltpu.VMEM(s, d) if n else jax.Sh...  46 us
    ppermute x10, waiting for transfers between devices, swap_x(): return lax.ppermute(value, 'fsdp', [(0, 1), (1, 0)])  19.5 us
    ppermute x10, starting transfers between devices, swap_x(): return lax.ppermute(value, 'fsdp', [(0, 1), (1, 0)])  11.7 us
    pallas_call x2, Pallas kernels, pack_call(): pl.pallas_call(kernel, out_shape=tuple((jax.ShapeDtypeStruct(s, bf16) for...  5.62 us
  transfers between devices with their start and end apart: 50, of which 25 were waited for; matrix products, arithmetic and copies ran while one was open for 0% of the time, Pallas kernels for 18%

profile of v2, /device:TPU:0, one launch (start us, length us, event | category | flops | bytes accessed | tf_op | source)
XLA Modules:
  0.0 200.1 jit_solution(10985803570334773681)
XLA Ops:
  3.8 2.9 %collective-permute-start = (bf16[1568,128]{1,0:T(8,128)(2,1)}, bf16[1568,128]{1,0:T(8,128)(2,1)S(1)}, u32[]{:S(2)}, u32[]{:S(2)}) collective-permute-start(bf16[1568,128]{1,0:T(8,128)(2,1)} %get-tuple-element.145), channel_id=1, source_target_pairs={{0,1},{1,0},{2,3},{3,2},{4,5},{5,4},{6,7},{7,6},{8,9},{9,8},{10,11... | collective-permute-start | bytes 1204232 | tf_op jit(solution)/shard_map/ppermute | solution.py:90
  6.8 3.1 %pack_tokens.1 = bf16[704,768]{1,0:T(8,128)(2,1)} custom-call(s32[4]{0:T(128)} %pad_add_fusion.ids.refs_0_, bf16[256,768]{1,0:T(8,128)(2,1)} %bitcast.9, bf16[256,768]{1,0:T(8,128)(2,1)} %bitcast.16, bf16[384,896]{1,0:T(8,128)(2,1)} %w.10), custom_call_target="tpu_custom_call" | custom-call | flops 1 | bytes 1 | tf_op jit(solution)/shard_map/pack_tokens/pallas_call | solution.py:194
  10.6 6.5 %collective-permute-done.pu = bf16[1568,128]{1,0:T(8,128)(2,1)S(1)} collective-permute-done((bf16[1568,128]{1,0:T(8,128)(2,1)}, bf16[1568,128]{1,0:T(8,128)(2,1)S(1)}, u32[]{:S(2)}, u32[]{:S(2)}) %collective-permute-start) | collective-permute-done | bytes 401440 | tf_op jit(solution)/shard_map/ppermute | solution.py:90
  23.2 2.7 %collective-permute-done.1.refs_1_ = bf16[256,128]{1,0:T(8,128)(2,1)S(1)} collective-permute-done((bf16[256,128]{1,0:T(8,128)(2,1)S(1)}, bf16[256,128]{1,0:T(8,128)(2,1)S(1)}, u32[]{:S(2)}, u32[]{:S(2)}) %collective-permute-start.1) | collective-permute-done | bytes 65568 | tf_op jit(solution)/shard_map/ppermute | solution.py:95
  27.9 3.0 %collective-permute-done.2.refs_1_ = bf16[512,128]{1,0:T(8,128)(2,1)S(1)} collective-permute-done((bf16[512,128]{1,0:T(8,128)(2,1)S(1)}, bf16[512,128]{1,0:T(8,128)(2,1)S(1)}, u32[]{:S(2)}, u32[]{:S(2)}) %collective-permute-start.2) | collective-permute-done | bytes 131104 | tf_op jit(solution)/shard_map/ppermute | solution.py:95
  31.3 6.1 %collective-permute-done.3.refs_1_ = bf16[1024,128]{1,0:T(8,128)(2,1)S(1)} collective-permute-done((bf16[1024,128]{1,0:T(8,128)(2,1)S(1)}, bf16[1024,128]{1,0:T(8,128)(2,1)S(1)}, u32[]{:S(2)}, u32[]{:S(2)}) %collective-permute-start.3) | collective-permute-done | bytes 262176 | tf_op jit(solution)/shard_map/ppermute | solution.py:95
  40.1 9.7 %ff.1 = (bf16[8,96,768]{2,1,0:T(8,128)(2,1)S(1)}, bf16[8,96,768]{2,1,0:T(8,128)(2,1)S(1)}, bf16[8,96,768]{2,1,0:T(8,128)(2,1)S(1)}, bf16[8,96,768]{2,1,0:T(8,128...) custom-call(s32[4]{0:T(128)S(1)} %copy-done.7, ...), custom_call_target="tpu_custom_call" | custom-call | flops 1 | bytes 1 | tf_op jit(solution)/shard_map/ff/pallas_call | solution.py:69
  59.6 3.6 %collective-permute-done.12.g_oth.refs_6_ = bf16[256,384]{1,0:T(8,128)(2,1)S(1)} collective-permute-done((bf16[256,384]{1,0:T(8,128)(2,1)S(1)}, bf16[256,384]{1,0:T(8,128)(2,1)S(1)}, u32[]{:S(2)}, u32[]{:S(2)}) %collective-permute-start.12) | collective-permute-done | bytes 196640 | tf_op jit(solution)/shard_map/ppermute | solution.py:90
  65.7 3.5 %collective-permute-done.13.b_ref = bf16[4,96,768]{2,1,0:T(8,128)(2,1)S(1)} collective-permute-done((bf16[4,96,768]{2,1,0:T(8,128)(2,1)S(1)}, bf16[4,96,768]{2,1,0:T(8,128)(2,1)S(1)}, u32[]{:S(2)}, u32[]{:S(2)}) %collective-permute-start.13) | collective-permute-done | bytes 589856 | tf_op jit(solution)/shard_map/ppermute | solution.py:95
  73.6 3.4 %collective-permute-done.14.b_ref = bf16[2,96,768]{2,1,0:T(8,128)(2,1)S(1)} collective-permute-done((bf16[2,96,768]{2,1,0:T(8,128)(2,1)S(1)}, bf16[2,96,768]{2,1,0:T(8,128)(2,1)S(1)}, u32[]{:S(2)}, u32[]{:S(2)}) %collective-permute-start.14) | collective-permute-done | bytes 294944 | tf_op jit(solution)/shard_map/ppermute | solution.py:95
  77.0 4.1 %collective-permute-done.15.b_ref = bf16[4,96,768]{2,1,0:T(8,128)(2,1)S(1)} collective-permute-done((bf16[4,96,768]{2,1,0:T(8,128)(2,1)S(1)}, bf16[4,96,768]{2,1,0:T(8,128)(2,1)S(1)}, u32[]{:S(2)}, u32[]{:S(2)}) %collective-permute-start.15) | collective-permute-done | bytes 589856 | tf_op jit(solution)/shard_map/ppermute | solution.py:95
  81.3 2.9 %collective-permute-start.17 = (bf16[1,96,768]{2,1,0:T(8,128)(2,1)S(1)}, bf16[1,96,768]{2,1,0:T(8,128)(2,1)S(1)}, u32[]{:S(2)}, u32[]{:S(2)}) collective-permute-start(bf16[1,96,768]{2,1,0:T(8,128)(2,1)S(1)} %get-tuple-element.198), channel_id=1, source_target_pairs={{0,16},{2,18},{4,20},{6,22},{8,24},{10,26},{12,28},{14,30},{16,0},... | collective-permute-start | bytes 442376 | tf_op jit(solution)/shard_map/ppermute | solution.py:95
  88.6 19.4 %collective-permute-start.18 = (bf16[2,96,768]{2,1,0:T(8,128)(2,1)S(1)}, bf16[2,96,768]{2,1,0:T(8,128)(2,1)S(1)}, u32[]{:S(2)}, u32[]{:S(2)}) collective-permute-start(bf16[2,96,768]{2,1,0:T(8,128)(2,1)S(1)} %get-tuple-element.200), channel_id=1, source_target_pairs={{0,8},{2,10},{4,12},{6,14},{8,0},{10,2},{12,4},{14,6},{16,24},{18,... | collective-permute-start | bytes 884744 | tf_op jit(solution)/shard_map/ppermute | solution.py:95
  110.5 2.6 %collective-permute-start.19 = (bf16[1024,128]{1,0:T(8,128)(2,1)S(1)}, bf16[1024,128]{1,0:T(8,128)(2,1)S(1)}, u32[]{:S(2)}, u32[]{:S(2)}) collective-permute-start(bf16[1024,128]{1,0:T(8,128)(2,1)S(1)} %get-tuple-element.207), channel_id=1, source_target_pairs={{0,4},{2,6},{4,0},{6,2},{8,12},{10,14},{12,8},{14,10},{16,20},{18,... | collective-permute-start | bytes 786440 | tf_op jit(solution)/shard_map/ppermute | solution.py:95
  116.1 5.5 %ff_rest.1 = (f32[256,768]{1,0:T(8,128)S(1)}, f32[256,768]{1,0:T(8,128)S(1)}, f32[256,768]{1,0:T(8,128)S(1)}, bf16[256,768]{1,0:T(8,128)(2,1)S(1)}, f32[8,128]{1,0:T(8,128)S(1)}, /*index=5*/f32[8,128]{1,0:T(8,128)S(1)}) custom-call(s32[4]{0:T(128)S(1)} %copy-done.7, bf16[512,1536]{1,0:T(8,128)(2,1)S(1)} %get-tuple-element.202.act, ...), custom_call_target="tpu_custom_call" | custom-call | flops 2000000000 | bytes 1 | tf_op jit(solution)/shard_map/ff_rest/pallas_call | solution.py:69
  127.6 3.1 %collective-permute-start.28 = (bf16[192,768]{1,0:T(8,128)(2,1)S(1)}, bf16[192,768]{1,0:T(8,128)(2,1)S(1)}, u32[]{:S(2)}, u32[]{:S(2)}) collective-permute-start(bf16[192,768]{1,0:T(8,128)(2,1)S(1)} %get-tuple-element.232), channel_id=1, source_target_pairs={{0,4},{2,6},{4,0},{6,2},{8,12},{10,14},{12,8},{14,10},{16,20},{18,... | collective-permute-start | bytes 884744 | tf_op jit(solution)/shard_map/ppermute | solution.py:95
  134.4 3.0 %collective-permute-done.26.other = bf16[1,96,384]{2,1,0:T(8,128)(2,1)S(1)} collective-permute-done((bf16[1,96,384]{2,1,0:T(8,128)(2,1)S(1)}, bf16[1,96,384]{2,1,0:T(8,128)(2,1)S(1)}, u32[]{:S(2)}, u32[]{:S(2)}) %collective-permute-start.26) | collective-permute-done | bytes 73760 | tf_op jit(solution)/shard_map/ppermute | solution.py:90
  137.5 3.6 %collective-permute-done.27.refs_1_ = bf16[256,128]{1,0:T(8,128)(2,1)S(1)} collective-permute-done((bf16[256,128]{1,0:T(8,128)(2,1)S(1)}, bf16[256,128]{1,0:T(8,128)(2,1)S(1)}, u32[]{:S(2)}, u32[]{:S(2)}) %collective-permute-start.27) | collective-permute-done | bytes 65568 | tf_op jit(solution)/shard_map/ppermute | solution.py:95
  160.7 3.7 %collective-permute-done.37.refs_1_ = bf16[2,96,768]{2,1,0:T(8,128)(2,1)S(1)} collective-permute-done((bf16[2,96,768]{2,1,0:T(8,128)(2,1)S(1)}, bf16[2,96,768]{2,1,0:T(8,128)(2,1)S(1)}, u32[]{:S(2)}, u32[]{:S(2)}) %collective-permute-start.37) | collective-permute-done | bytes 294944 | tf_op jit(solution)/shard_map/ppermute | solution.py:95
  170.4 4.1 %collective-permute-done.42.refs_1_ = bf16[96,768]{1,0:T(8,128)(2,1)S(1)} collective-permute-done((bf16[96,768]{1,0:T(8,128)(2,1)S(1)}, bf16[96,768]{1,0:T(8,128)(2,1)S(1)}, u32[]{:S(2)}, u32[]{:S(2)}) %collective-permute-start.42) | collective-permute-done | bytes 147488 | tf_op jit(solution)/shard_map/ppermute | solution.py:95
  175.7 3.8 %collective-permute-done.44.refs_1_ = bf16[4,96,768]{2,1,0:T(8,128)(2,1)S(1)} collective-permute-done((bf16[4,96,768]{2,1,0:T(8,128)(2,1)S(1)}, bf16[4,96,768]{2,1,0:T(8,128)(2,1)S(1)}, u32[]{:S(2)}, u32[]{:S(2)}) %collective-permute-start.44) | collective-permute-done | bytes 589856 | tf_op jit(solution)/shard_map/ppermute | solution.py:95
  182.7 6.9 %collective-permute-done.45.refs_1_ = bf16[416,128]{1,0:T(8,128)(2,1)S(1)} collective-permute-done((bf16[416,128]{1,0:T(8,128)(2,1)S(1)}, bf16[416,128]{1,0:T(8,128)(2,1)S(1)}, u32[]{:S(2)}, u32[]{:S(2)}) %collective-permute-start.45) | collective-permute-done | bytes 106528 | tf_op jit(solution)/shard_map/ppermute | solution.py:95
  194.0 3.0 %down_out.1 = f32[1536,768]{1,0:T(8,128)} custom-call(s32[4]{0:T(128)S(1)} %copy-done.7, bf16[8,96,768]{2,1,0:T(8,128)(2,1)S(1)} %down_join.5.mine, bf16[8,96,768]{2,1,0:T(8,128)(2,1)S(1)} %collective-permute-done.48.theirs), custom_call_target="tpu_custom_call" | custom-call | flops 1 | bytes 1 | tf_op jit(solution)/shard_map/down_out/pallas_call | solution.py:69
  197.1 3.0 %up_out.1 = f32[384,3072]{1,0:T(8,128)} custom-call(s32[4]{0:T(128)S(1)} %copy-done.7, bf16[8,96,768]{2,1,0:T(8,128)(2,1)S(1)} %up_join.7.mine, bf16[8,96,768]{2,1,0:T(8,128)(2,1)S(1)} %collective-permute-done.49.theirs), custom_call_target="tpu_custom_call" | custom-call | flops 1 | bytes 1 | tf_op jit(solution)/shard_map/up_out/pallas_call | solution.py:69
  (169 shorter events, 85.6 us)
Async XLA Ops:
  3.8 13.3 %collective-permute-start = (bf16[1568,128]{1,0:T(8,128)(2,1)}, bf16[1568,128]{1,0:T(8,128)(2,1)S(1)}, u32[]{:S(2)}, u32[]{:S(2)}) collective-permute-start(bf16[1568,128]{1,0:T(8,128)(2,1)} %get-tuple-element.145), channel_id=1, source_target_pairs={{0,1},{1,0},{2,3},{3,2},{4,5},{5,4},{6,7},{7,6},{8,9},{9,8},{10,11... | collective-permute-start | bytes 1204232 | tf_op jit(solution)/shard_map/ppermute | solution.py:90
  9.9 29.6 %collective-permute-start.4 = (bf16[704,768]{1,0:T(8,128)(2,1)}, bf16[704,768]{1,0:T(8,128)(2,1)S(1)}, u32[]{:S(2)}, u32[]{:S(2)}) collective-permute-start(bf16[704,768]{1,0:T(8,128)(2,1)} %pack_tokens.1), channel_id=1, source_target_pairs={{0,1},{1,0},{2,3},{3,2},{4,5},{5,4},{6,7},{7,6},{8,9},{9,8},{10,11... | collective-permute-start | bytes 3244040 | tf_op jit(solution)/shard_map/ppermute | solution.py:90
  18.4 9.0 %collective-permute-start.5 = (bf16[384,384]{1,0:T(8,128)(2,1)S(1)}, bf16[384,384]{1,0:T(8,128)(2,1)S(1)}, u32[]{:S(2)}, u32[]{:S(2)}) collective-permute-start(bf16[384,384]{1,0:T(8,128)(2,1)S(1)} %get-tuple-element.155.up0), channel_id=1, source_target_pairs={{0,4},{2,6},{4,0},{6,2},{8,12},{10,14},{12,8},{14,10},{16,20},{18,... | collective-permute-start | bytes 884744 | tf_op jit(solution)/shard_map/ppermute | solution.py:95
  27.4 12.6 %collective-permute-start.6 = (bf16[384,384]{1,0:T(8,128)(2,1)S(1)}, bf16[384,384]{1,0:T(8,128)(2,1)S(1)}, u32[]{:S(2)}, u32[]{:S(2)}) collective-permute-start(bf16[384,384]{1,0:T(8,128)(2,1)S(1)} %get-tuple-element.155.up0), channel_id=1, source_target_pairs={{0,2},{2,0},{4,6},{6,4},{8,10},{10,8},{12,14},{14,12},{16,18},{18,... | collective-permute-start | bytes 884744 | tf_op jit(solution)/shard_map/ppermute | solution.py:95
  27.4 12.6 %collective-permute-start.7 = (bf16[384,384]{1,0:T(8,128)(2,1)S(1)}, bf16[384,384]{1,0:T(8,128)(2,1)S(1)}, u32[]{:S(2)}, u32[]{:S(2)}) collective-permute-start(bf16[384,384]{1,0:T(8,128)(2,1)S(1)} %collective-permute-done.5.up1), channel_id=1, source_target_pairs={{0,2},{2,0},{4,6},{6,4},{8,10},{10,8},{12,14},{14,12},{16,18},{18,... | collective-permute-start | bytes 884744 | tf_op jit(solution)/shard_map/ppermute | solution.py:95
  53.0 16.2 %collective-permute-start.13 = (bf16[4,96,768]{2,1,0:T(8,128)(2,1)S(1)}, bf16[4,96,768]{2,1,0:T(8,128)(2,1)S(1)}, u32[]{:S(2)}, u32[]{:S(2)}) collective-permute-start(bf16[4,96,768]{2,1,0:T(8,128)(2,1)S(1)} %get-tuple-element.171), channel_id=1, source_target_pairs={{0,4},{2,6},{4,0},{6,2},{8,12},{10,14},{12,8},{14,10},{16,20},{18,... | collective-permute-start | bytes 1769480 | tf_op jit(solution)/shard_map/ppermute | solution.py:95
  55.6 25.5 %collective-permute-start.15 = (bf16[4,96,768]{2,1,0:T(8,128)(2,1)S(1)}, bf16[4,96,768]{2,1,0:T(8,128)(2,1)S(1)}, u32[]{:S(2)}, u32[]{:S(2)}) collective-permute-start(bf16[4,96,768]{2,1,0:T(8,128)(2,1)S(1)} %get-tuple-element.180), channel_id=1, source_target_pairs={{0,4},{2,6},{4,0},{6,2},{8,12},{10,14},{12,8},{14,10},{16,20},{18,... | collective-permute-start | bytes 1769480 | tf_op jit(solution)/shard_map/ppermute | solution.py:95
  81.3 29.1 %collective-permute-start.17 = (bf16[1,96,768]{2,1,0:T(8,128)(2,1)S(1)}, bf16[1,96,768]{2,1,0:T(8,128)(2,1)S(1)}, u32[]{:S(2)}, u32[]{:S(2)}) collective-permute-start(bf16[1,96,768]{2,1,0:T(8,128)(2,1)S(1)} %get-tuple-element.198), channel_id=1, source_target_pairs={{0,16},{2,18},{4,20},{6,22},{8,24},{10,26},{12,28},{14,30},{16,0},... | collective-permute-start | bytes 442376 | tf_op jit(solution)/shard_map/ppermute | solution.py:95
  88.6 25.1 %collective-permute-start.18 = (bf16[2,96,768]{2,1,0:T(8,128)(2,1)S(1)}, bf16[2,96,768]{2,1,0:T(8,128)(2,1)S(1)}, u32[]{:S(2)}, u32[]{:S(2)}) collective-permute-start(bf16[2,96,768]{2,1,0:T(8,128)(2,1)S(1)} %get-tuple-element.200), channel_id=1, source_target_pairs={{0,8},{2,10},{4,12},{6,14},{8,0},{10,2},{12,4},{14,6},{16,24},{18,... | collective-permute-start | bytes 884744 | tf_op jit(solution)/shard_map/ppermute | solution.py:95
  108.1 15.8 %collective-permute-start.20 = (bf16[256,768]{1,0:T(8,128)(2,1)S(1)}, bf16[256,768]{1,0:T(8,128)(2,1)S(1)}, u32[]{:S(2)}, u32[]{:S(2)}) collective-permute-start(bf16[256,768]{1,0:T(8,128)(2,1)S(1)} %get-tuple-element.211.dm_own.dm), channel_id=1, source_target_pairs={{0,1},{1,0},{2,3},{3,2},{4,5},{5,4},{6,7},{7,6},{8,9},{9,8},{10,11... | collective-permute-start | bytes 1179656 | tf_op jit(solution)/shard_map/ppermute | solution.py:90
  108.3 15.7 %collective-permute-start.21 = (bf16[256,384]{1,0:T(8,128)(2,1)S(1)}, bf16[256,384]{1,0:T(8,128)(2,1)S(1)}, u32[]{:S(2)}, u32[]{:S(2)}) collective-permute-start(bf16[256,384]{1,0:T(8,128)(2,1)S(1)} %get-tuple-element.212), channel_id=1, source_target_pairs={{0,1},{1,0},{2,3},{3,2},{4,5},{5,4},{6,7},{7,6},{8,9},{9,8},{10,11... | collective-permute-start | bytes 589832 | tf_op jit(solution)/shard_map/ppermute | solution.py:90
  110.4 16.0 %collective-permute-start.23 = (bf16[1,96,768]{2,1,0:T(8,128)(2,1)S(1)}, bf16[1,96,768]{2,1,0:T(8,128)(2,1)S(1)}, u32[]{:S(2)}, u32[]{:S(2)}) collective-permute-start(bf16[1,96,768]{2,1,0:T(8,128)(2,1)S(1)} %down_sum.1.refs_0_), channel_id=1, source_target_pairs={{0,16},{2,18},{4,20},{6,22},{8,24},{10,26},{12,28},{14,30},{16,0},... | collective-permute-start | bytes 442376 | tf_op jit(solution)/shard_map/ppermute | solution.py:95
  110.5 11.1 %collective-permute-start.19 = (bf16[1024,128]{1,0:T(8,128)(2,1)S(1)}, bf16[1024,128]{1,0:T(8,128)(2,1)S(1)}, u32[]{:S(2)}, u32[]{:S(2)}) collective-permute-start(bf16[1024,128]{1,0:T(8,128)(2,1)S(1)} %get-tuple-element.207), channel_id=1, source_target_pairs={{0,4},{2,6},{4,0},{6,2},{8,12},{10,14},{12,8},{14,10},{16,20},{18,... | collective-permute-start | bytes 786440 | tf_op jit(solution)/shard_map/ppermute | solution.py:95
  113.8 12.5 %collective-permute-start.22 = (bf16[1,96,768]{2,1,0:T(8,128)(2,1)S(1)}, bf16[1,96,768]{2,1,0:T(8,128)(2,1)S(1)}, u32[]{:S(2)}, u32[]{:S(2)}) collective-permute-start(bf16[1,96,768]{2,1,0:T(8,128)(2,1)S(1)} %get-tuple-element.217), channel_id=1, source_target_pairs={{0,16},{2,18},{4,20},{6,22},{8,24},{10,26},{12,28},{14,30},{16,0},... | collective-permute-start | bytes 442376 | tf_op jit(solution)/shard_map/ppermute | solution.py:95
  127.6 13.6 %collective-permute-start.28 = (bf16[192,768]{1,0:T(8,128)(2,1)S(1)}, bf16[192,768]{1,0:T(8,128)(2,1)S(1)}, u32[]{:S(2)}, u32[]{:S(2)}) collective-permute-start(bf16[192,768]{1,0:T(8,128)(2,1)S(1)} %get-tuple-element.232), channel_id=1, source_target_pairs={{0,4},{2,6},{4,0},{6,2},{8,12},{10,14},{12,8},{14,10},{16,20},{18,... | collective-permute-start | bytes 884744 | tf_op jit(solution)/shard_map/ppermute | solution.py:95
  130.8 12.0 %collective-permute-start.29 = (bf16[2,96,768]{2,1,0:T(8,128)(2,1)S(1)}, bf16[2,96,768]{2,1,0:T(8,128)(2,1)S(1)}, u32[]{:S(2)}, u32[]{:S(2)}) collective-permute-start(bf16[2,96,768]{2,1,0:T(8,128)(2,1)S(1)} %down_join.3.refs_0_), channel_id=1, source_target_pairs={{0,8},{2,10},{4,12},{6,14},{8,0},{10,2},{12,4},{14,6},{16,24},{18,... | collective-permute-start | bytes 884744 | tf_op jit(solution)/shard_map/ppermute | solution.py:95
  132.6 20.6 %collective-permute-start.34 = (bf16[256,768]{1,0:T(8,128)(2,1)S(1)}, bf16[256,768]{1,0:T(8,128)(2,1)S(1)}, u32[]{:S(2)}, u32[]{:S(2)}) collective-permute-start(bf16[256,768]{1,0:T(8,128)(2,1)S(1)} %get-tuple-element.247), channel_id=1, source_target_pairs={{0,1},{1,0},{2,3},{3,2},{4,5},{5,4},{6,7},{7,6},{8,9},{9,8},{10,11... | collective-permute-start | bytes 1179656 | tf_op jit(solution)/shard_map/ppermute | solution.py:90
  142.8 25.4 %collective-permute-start.40 = (bf16[4,96,768]{2,1,0:T(8,128)(2,1)S(1)}, bf16[4,96,768]{2,1,0:T(8,128)(2,1)S(1)}, u32[]{:S(2)}, u32[]{:S(2)}) collective-permute-start(bf16[4,96,768]{2,1,0:T(8,128)(2,1)S(1)} %down_join.4.refs_0_), channel_id=1, source_target_pairs={{0,4},{2,6},{4,0},{6,2},{8,12},{10,14},{12,8},{14,10},{16,20},{18,... | collective-permute-start | bytes 1769480 | tf_op jit(solution)/shard_map/ppermute | solution.py:95
  152.9 13.6 %collective-permute-start.39 = (bf16[256,768]{1,0:T(8,128)(2,1)S(1)}, bf16[256,768]{1,0:T(8,128)(2,1)S(1)}, u32[]{:S(2)}, u32[]{:S(2)}) collective-permute-start(bf16[256,768]{1,0:T(8,128)(2,1)S(1)} %mix.1), channel_id=1, source_target_pairs={{0,1},{1,0},{2,3},{3,2},{4,5},{5,4},{6,7},{7,6},{8,9},{9,8},{10,11... | collective-permute-start | bytes 1179656 | tf_op jit(solution)/shard_map/ppermute | solution.py:90
  153.2 11.3 %collective-permute-start.37 = (bf16[2,96,768]{2,1,0:T(8,128)(2,1)S(1)}, bf16[2,96,768]{2,1,0:T(8,128)(2,1)S(1)}, u32[]{:S(2)}, u32[]{:S(2)}) collective-permute-start(bf16[2,96,768]{2,1,0:T(8,128)(2,1)S(1)} %up_join.5.refs_0_), channel_id=1, source_target_pairs={{0,8},{2,10},{4,12},{6,14},{8,0},{10,2},{12,4},{14,6},{16,24},{18,... | collective-permute-start | bytes 884744 | tf_op jit(solution)/shard_map/ppermute | solution.py:95
  164.5 14.9 %collective-permute-start.44 = (bf16[4,96,768]{2,1,0:T(8,128)(2,1)S(1)}, bf16[4,96,768]{2,1,0:T(8,128)(2,1)S(1)}, u32[]{:S(2)}, u32[]{:S(2)}) collective-permute-start(bf16[4,96,768]{2,1,0:T(8,128)(2,1)S(1)} %up_join.6.refs_0_), channel_id=1, source_target_pairs={{0,4},{2,6},{4,0},{6,2},{8,12},{10,14},{12,8},{14,10},{16,20},{18,... | collective-permute-start | bytes 1769480 | tf_op jit(solution)/shard_map/ppermute | solution.py:95
  170.4 23.6 %collective-permute-start.48 = (bf16[8,96,768]{2,1,0:T(8,128)(2,1)S(1)}, bf16[8,96,768]{2,1,0:T(8,128)(2,1)S(1)}, u32[]{:S(2)}, u32[]{:S(2)}) collective-permute-start(bf16[8,96,768]{2,1,0:T(8,128)(2,1)S(1)} %down_join.5.mine), channel_id=1, source_target_pairs={{0,2},{2,0},{4,6},{6,4},{8,10},{10,8},{12,14},{14,12},{16,18},{18,... | collective-permute-start | bytes 3538952 | tf_op jit(solution)/shard_map/ppermute | solution.py:95
  179.5 17.6 %collective-permute-start.49 = (bf16[8,96,768]{2,1,0:T(8,128)(2,1)S(1)}, bf16[8,96,768]{2,1,0:T(8,128)(2,1)S(1)}, u32[]{:S(2)}, u32[]{:S(2)}) collective-permute-start(bf16[8,96,768]{2,1,0:T(8,128)(2,1)S(1)} %up_join.7.mine), channel_id=1, source_target_pairs={{0,2},{2,0},{4,6},{6,4},{8,10},{10,8},{12,14},{14,12},{16,18},{18,... | collective-permute-start | bytes 3538952 | tf_op jit(solution)/shard_map/ppermute | solution.py:95
  179.6 10.1 %collective-permute-start.46 = (bf16[192,768]{1,0:T(8,128)(2,1)S(1)}, bf16[192,768]{1,0:T(8,128)(2,1)S(1)}, u32[]{:S(2)}, u32[]{:S(2)}) collective-permute-start(bf16[192,768]{1,0:T(8,128)(2,1)S(1)} %pair_join.4.refs_0_), channel_id=1, source_target_pairs={{0,4},{2,6},{4,0},{6,2},{8,12},{10,14},{12,8},{14,10},{16,20},{18,... | collective-permute-start | bytes 884744 | tf_op jit(solution)/shard_map/ppermute | solution.py:95
  (40 other events, 304.1 us)
